TPU v7x, 32 devices: a whole 2x2x4 slice. The times are simulated.
32 devices in a mesh: dp: 8 (over z, x), fsdp: 4 (over y, core).
Axes of the slice: x: 2, y: 2, z: 4, core: 2. Of those that a mesh axis runs over, the one named last changes fastest.
Arguments:
- tokens: bfloat16 [2, 16, 1024, 768], P(None, 'dp', 'fsdp'), may hold values from -6 to 6
- cotangent: bfloat16 [2, 16, 1024, 768], P(None, 'dp', 'fsdp'), may hold values from -6 to 6
- lengths: int32 [2, 16], P(None, 'dp'), may hold values from 256 to 1024, as said below
- inward_weight: float32 [768, 2304], P('fsdp'), may hold values from -0.21875 to 0.21875
- outward_weight: float32 [768, 768], P('fsdp'), may hold values from -6 to 6
- expand_weight: float32 [768, 2304], P('fsdp'), may hold values from -0.21875 to 0.21875
- shrink_weight: float32 [1152, 768], P('fsdp'), may hold values from -0.1875 to 0.1875
- gain_weight: float32 [2, 768], P(None, 'fsdp'), may hold values from 0.5 to 1.5
- inward_first: float32 [768, 2304], P('fsdp'), may hold values from -2048 to 2048
- outward_first: float32 [768, 768], P('fsdp'), may hold values from -64 to 64
- expand_first: float32 [768, 2304], P('fsdp'), may hold values from -512 to 512
- shrink_first: float32 [1152, 768], P('fsdp'), may hold values from -512 to 512
- gain_first: float32 [2, 768], P(None, 'fsdp'), may hold values from -2048 to 2048
- inward_second: float32 [768, 2304], P('fsdp'), may hold values from 104857.6 to 419430.4
- outward_second: float32 [768, 768], P('fsdp'), may hold values from 131.072 to 524.288
- expand_second: float32 [768, 2304], P('fsdp'), may hold values from 6553.6 to 26214.4
- shrink_second: float32 [1152, 768], P('fsdp'), may hold values from 9502.72 to 38010.88
- gain_second: float32 [2, 768], P(None, 'fsdp'), may hold values from 104857.6 to 419430.4
Outputs:
- block_out: bfloat16 [2, 16, 1024, 768], P(None, 'dp', 'fsdp')
- input_grad: float32 [2, 16, 1024, 768], P(None, 'dp', 'fsdp')
- inward_renewed: float32 [768, 2304], P('fsdp')
- inward_momentum: float32 [768, 2304], P('fsdp')
- inward_variance: float32 [768, 2304], P('fsdp')
- outward_renewed: float32 [768, 768], P('fsdp')
- outward_momentum: float32 [768, 768], P('fsdp')
- outward_variance: float32 [768, 768], P('fsdp')
- expand_renewed: float32 [768, 2304], P('fsdp')
- expand_momentum: float32 [768, 2304], P('fsdp')
- expand_variance: float32 [768, 2304], P('fsdp')
- shrink_renewed: float32 [1152, 768], P('fsdp')
- shrink_momentum: float32 [1152, 768], P('fsdp')
- shrink_variance: float32 [1152, 768], P('fsdp')
- gain_renewed: float32 [2, 768], P(None, 'fsdp')
- gain_momentum: float32 [2, 768], P(None, 'fsdp')
- gain_variance: float32 [2, 768], P(None, 'fsdp')
Inputs may be any that keep to these rules, and one draw needn't show every extreme that they name: `lengths`: in each micro-batch, among the 2 sequences of each dp index, one has length 1024.
All inputs are finite; a program needn't handle non-finite values.
Results may differ from a plain program's by a relative error of at most 0.014.
Values may be sent and summed in bfloat16 or wider, within the bound.
No kernel may reach another device: no remote copies, remote signals or barrier semaphores. Data moves between devices by JAX's collectives and lax.ppermute only.
A program may use at most 256 MiB of HBM per device.

v0:
```python
import jax
import jax.numpy as jnp
from jax import lax
from jax.sharding import PartitionSpec as P

FF = 1152
HEADS = 12
HDIM = 64
STEP = 10


rope_base = 160000.0
norm_eps = 1e-05
adam_beta = 0.5
adam_eps = 1e-08
weight_decay = 0.01
rates = (0.07, 2.0, 0.07, 0.06, 0.2)
masked_score = -1e30


def tables(positions):
    half_dim = HDIM // 2
    exponent = jnp.arange(half_dim, dtype=jnp.float32) * (2.0 / HDIM)
    inverse = jnp.power(jnp.float32(rope_base), -exponent)
    angles = positions.astype(jnp.float32)[:, None] * inverse[None, :]
    return (jnp.cos(angles), jnp.sin(angles))


def rotate(values, cosine, sine_table):
    half_dim = values.shape[-1] // 2
    former = values[..., :half_dim]
    latter = values[..., half_dim:]
    cos_wide = cosine[:, None, :]
    sin_wide = sine_table[:, None, :]
    return jnp.concatenate(
        [former * cos_wide - latter * sin_wide, latter * cos_wide + former * sin_wide], axis=-1
    )


def normalize(values, gain_row):
    center = values - jnp.mean(values, axis=-1, keepdims=True)
    spread = jnp.mean(center * center, axis=-1, keepdims=True)
    return center * lax.rsqrt(spread + norm_eps) * gain_row


def geglu(joined_heads):
    gate_part = joined_heads[..., :FF]
    upward = joined_heads[..., FF:]
    return 0.5 * gate_part * (1.0 + lax.erf(gate_part * 0.7071067811865476)) * upward


def attention_scores(queries, keys_all, live_keys, score_scale):
    product = (
        jnp.einsum("sqhd,skhd->shqk", queries, keys_all, preferred_element_type=jnp.float32)
        * score_scale
    )
    return jnp.where(live_keys[:, None, None, :], product, masked_score)


def adam_update(master, gradient, moment_one, moment_two, step_rate, decay_rate):
    first_new = adam_beta * moment_one + (1.0 - adam_beta) * gradient
    second_new = adam_beta * moment_two + (1.0 - adam_beta) * gradient * gradient
    correction = 1.0 - adam_beta**STEP
    direction = first_new / correction / (jnp.sqrt(second_new / correction) + adam_eps)
    renewed = master - step_rate * (direction + decay_rate * master)
    return (renewed, first_new, second_new)


def local(
    tokens,
    cotangent,
    lengths,
    inward_weight,
    outward_weight,
    expand_weight,
    shrink_weight,
    gain_weight,
    inward_first,
    outward_first,
    expand_first,
    shrink_first,
    gain_first,
    inward_second,
    outward_second,
    expand_second,
    shrink_second,
    gain_second,
):
    micro_count, group_size, local_len, model_width = tokens.shape
    seq_total = local_len * lax.axis_size("fsdp")
    row_count = group_size * local_len
    score_scale = HDIM ** (-0.5)
    positions = lax.axis_index("fsdp") * local_len + jnp.arange(local_len, dtype=jnp.int32)
    cosine, sine_table = tables(positions)
    key_positions = jnp.arange(seq_total, dtype=jnp.int32)
    inward_copy = inward_weight.astype(jnp.bfloat16)
    outward_copy = outward_weight.astype(jnp.bfloat16)
    expand_copy = expand_weight.astype(jnp.bfloat16)
    shrink_copy = shrink_weight.astype(jnp.bfloat16)
    gain_copy = gain_weight.astype(jnp.bfloat16)
    accum = (
        jnp.zeros((model_width, 3 * model_width), jnp.float32),
        jnp.zeros((model_width, model_width), jnp.float32),
        jnp.zeros((model_width, 2 * FF), jnp.float32),
        jnp.zeros((FF, model_width), jnp.float32),
        jnp.zeros((2, model_width), jnp.float32),
    )

    def micro_step(accum, item):
        input_tokens, incoming, limits = item
        gathered = (
            lax.all_gather(inward_copy, "fsdp", axis=0, tiled=True),
            lax.all_gather(outward_copy, "fsdp", axis=0, tiled=True),
            lax.all_gather(expand_copy, "fsdp", axis=0, tiled=True),
            lax.all_gather(shrink_copy, "fsdp", axis=0, tiled=True),
            lax.all_gather(gain_copy, "fsdp", axis=1, tiled=True),
        )
        inward_matrix, outward_matrix, expand_matrix, shrink_matrix, gain_full = gathered
        gain_rows = gain_full.astype(jnp.float32)
        live_keys = key_positions[None, :] < limits[:, None]
        live_rows = (positions[None, :] < limits[:, None]).astype(jnp.float32).reshape(row_count, 1)
        flat_in = input_tokens.astype(jnp.float32).reshape(row_count, model_width)
        hidden_first_norm = normalize(flat_in, gain_rows[0]).astype(jnp.bfloat16)
        joined_heads = jnp.dot(
            hidden_first_norm, inward_matrix, preferred_element_type=jnp.float32
        ).reshape(group_size, local_len, 3, HEADS, HDIM)
        queries = rotate(joined_heads[:, :, 0], cosine, sine_table).astype(jnp.bfloat16)
        keys_local = rotate(joined_heads[:, :, 1], cosine, sine_table).astype(jnp.bfloat16)
        values_local = joined_heads[:, :, 2].astype(jnp.bfloat16)
        keys_all, values_all = (
            lax.all_gather(keys_local, "fsdp", axis=1, tiled=True),
            lax.all_gather(values_local, "fsdp", axis=1, tiled=True),
        )
        scores = attention_scores(queries, keys_all, live_keys, score_scale)
        row_peak = jnp.max(scores, axis=-1, keepdims=True)
        exp_terms = jnp.exp(scores - row_peak)
        totals = jnp.sum(exp_terms, axis=-1, keepdims=True)
        attention_low = (exp_terms / totals).astype(jnp.bfloat16)
        log_total = row_peak + jnp.log(totals)
        mixed_tokens = jnp.einsum(
            "shqk,skhd->sqhd", attention_low, values_all, preferred_element_type=jnp.float32
        )
        mixed_tokens = mixed_tokens.astype(jnp.bfloat16).reshape(row_count, model_width)
        middle_state = flat_in + jnp.dot(
            mixed_tokens, outward_matrix, preferred_element_type=jnp.float32
        )
        hidden_second_norm = normalize(middle_state, gain_rows[1]).astype(jnp.bfloat16)
        expanded_rows = jnp.dot(
            hidden_second_norm, expand_matrix, preferred_element_type=jnp.float32
        )
        hidden_state = geglu(expanded_rows).astype(jnp.bfloat16)
        layer_result = (
            middle_state + jnp.dot(hidden_state, shrink_matrix, preferred_element_type=jnp.float32)
        ) * live_rows
        block_rows = layer_result.astype(jnp.bfloat16).reshape(group_size, local_len, model_width)
        gathered_back = (
            lax.all_gather(inward_copy, "fsdp", axis=0, tiled=True),
            lax.all_gather(outward_copy, "fsdp", axis=0, tiled=True),
            lax.all_gather(expand_copy, "fsdp", axis=0, tiled=True),
            lax.all_gather(shrink_copy, "fsdp", axis=0, tiled=True),
            lax.all_gather(gain_copy, "fsdp", axis=1, tiled=True),
        )
        inward_back, outward_back, expand_back, shrink_back, gain_back = gathered_back
        gain_rows_back = gain_back.astype(jnp.float32)
        grad_out = incoming.astype(jnp.float32).reshape(row_count, model_width) * live_rows
        branch_low = grad_out.astype(jnp.bfloat16)
        shrink_grad = jnp.einsum(
            "rf,rd->fd", hidden_state, branch_low, preferred_element_type=jnp.float32
        )
        hidden_grad = jnp.einsum(
            "rd,fd->rf", branch_low, shrink_back, preferred_element_type=jnp.float32
        )
        unused, geglu_back = jax.vjp(geglu, expanded_rows)
        expanded_grad = geglu_back(hidden_grad)[0].astype(jnp.bfloat16)
        expand_grad = jnp.einsum(
            "rd,re->de", hidden_second_norm, expanded_grad, preferred_element_type=jnp.float32
        )
        h_two_grad = jnp.einsum(
            "re,de->rd", expanded_grad, expand_back, preferred_element_type=jnp.float32
        )
        unused, second_back = jax.vjp(normalize, middle_state, gain_rows_back[1])
        middle_part, gain_two_grad = second_back(h_two_grad)
        middle_grad = grad_out + middle_part
        mixer_low = middle_grad.astype(jnp.bfloat16)
        outward_grad = jnp.einsum(
            "rd,re->de", mixed_tokens, mixer_low, preferred_element_type=jnp.float32
        )
        mixed_grad = jnp.einsum(
            "re,de->rd", mixer_low, outward_back, preferred_element_type=jnp.float32
        )
        mixed_grad = mixed_grad.astype(jnp.bfloat16).reshape(group_size, local_len, HEADS, HDIM)
        scores_again = attention_scores(queries, keys_all, live_keys, score_scale)
        attention = jnp.exp(scores_again - log_total)
        attention_again = attention.astype(jnp.bfloat16)
        attention_grad = jnp.einsum(
            "sqhd,skhd->shqk", mixed_grad, values_all, preferred_element_type=jnp.float32
        )
        row_inner = jnp.sum(attention * attention_grad, axis=-1, keepdims=True)
        score_grad = (attention * (attention_grad - row_inner)).astype(jnp.bfloat16)
        query_grad = (
            jnp.einsum("shqk,skhd->sqhd", score_grad, keys_all, preferred_element_type=jnp.float32)
            * score_scale
        )
        key_part = (
            jnp.einsum("shqk,sqhd->skhd", score_grad, queries, preferred_element_type=jnp.float32)
            * score_scale
        )
        value_part = jnp.einsum(
            "shqk,sqhd->skhd", attention_again, mixed_grad, preferred_element_type=jnp.float32
        )
        key_grad, value_grad = (
            lax.psum_scatter(
                key_part.astype(jnp.bfloat16), "fsdp", scatter_dimension=1, tiled=True
            ).astype(jnp.float32),
            lax.psum_scatter(
                value_part.astype(jnp.bfloat16), "fsdp", scatter_dimension=1, tiled=True
            ).astype(jnp.float32),
        )
        joined_grad = jnp.stack(
            [
                rotate(query_grad, cosine, -sine_table),
                rotate(key_grad, cosine, -sine_table),
                value_grad,
            ],
            axis=2,
        )
        joined_grad = joined_grad.reshape(row_count, 3 * model_width).astype(jnp.bfloat16)
        inward_grad = jnp.einsum(
            "rd,re->de", hidden_first_norm, joined_grad, preferred_element_type=jnp.float32
        )
        h_one_grad = jnp.einsum(
            "re,de->rd", joined_grad, inward_back, preferred_element_type=jnp.float32
        )
        unused, first_back = jax.vjp(normalize, flat_in, gain_rows_back[0])
        input_part, gain_one_grad = first_back(h_one_grad)
        input_rows = (middle_grad + input_part).reshape(group_size, local_len, model_width)
        gain_grad = jnp.stack([gain_one_grad, gain_two_grad])
        accum = jax.tree.map(
            jnp.add, accum, (inward_grad, outward_grad, expand_grad, shrink_grad, gain_grad)
        )
        return (accum, (block_rows, input_rows))

    accum, outputs = lax.scan(micro_step, accum, (tokens, cotangent, lengths))
    block_out, input_grad = outputs
    shards = (
        lax.psum_scatter(
            accum[0].astype(jnp.bfloat16), "fsdp", scatter_dimension=0, tiled=True
        ).astype(jnp.float32),
        lax.psum_scatter(
            accum[1].astype(jnp.bfloat16), "fsdp", scatter_dimension=0, tiled=True
        ).astype(jnp.float32),
        lax.psum_scatter(
            accum[2].astype(jnp.bfloat16), "fsdp", scatter_dimension=0, tiled=True
        ).astype(jnp.float32),
        lax.psum_scatter(
            accum[3].astype(jnp.bfloat16), "fsdp", scatter_dimension=0, tiled=True
        ).astype(jnp.float32),
        lax.psum_scatter(
            accum[4].astype(jnp.bfloat16), "fsdp", scatter_dimension=1, tiled=True
        ).astype(jnp.float32),
    )
    shards = lax.psum((shards[0], shards[1], shards[2], shards[3], shards[4]), "dp")
    inward_new = adam_update(
        inward_weight, shards[0], inward_first, inward_second, rates[0], weight_decay
    )
    outward_new = adam_update(
        outward_weight, shards[1], outward_first, outward_second, rates[1], weight_decay
    )
    expand_new = adam_update(
        expand_weight, shards[2], expand_first, expand_second, rates[2], weight_decay
    )
    shrink_new = adam_update(
        shrink_weight, shards[3], shrink_first, shrink_second, rates[3], weight_decay
    )
    gain_new = adam_update(gain_weight, shards[4], gain_first, gain_second, rates[4], 0.0)
    return (
        block_out,
        input_grad,
        inward_new[0],
        inward_new[1],
        inward_new[2],
        outward_new[0],
        outward_new[1],
        outward_new[2],
        expand_new[0],
        expand_new[1],
        expand_new[2],
        shrink_new[0],
        shrink_new[1],
        shrink_new[2],
        gain_new[0],
        gain_new[1],
        gain_new[2],
    )


def solution(mesh):
    in_specs = (
        P(None, "dp", "fsdp", None),
        P(None, "dp", "fsdp", None),
        P(None, "dp"),
        P("fsdp", None),
        P("fsdp", None),
        P("fsdp", None),
        P("fsdp", None),
        P(None, "fsdp"),
        P("fsdp", None),
        P("fsdp", None),
        P("fsdp", None),
        P("fsdp", None),
        P(None, "fsdp"),
        P("fsdp", None),
        P("fsdp", None),
        P("fsdp", None),
        P("fsdp", None),
        P(None, "fsdp"),
    )
    out_specs = (
        P(None, "dp", "fsdp", None),
        P(None, "dp", "fsdp", None),
        P("fsdp", None),
        P("fsdp", None),
        P("fsdp", None),
        P("fsdp", None),
        P("fsdp", None),
        P("fsdp", None),
        P("fsdp", None),
        P("fsdp", None),
        P("fsdp", None),
        P("fsdp", None),
        P("fsdp", None),
        P("fsdp", None),
        P(None, "fsdp"),
        P(None, "fsdp"),
        P(None, "fsdp"),
    )
    return jax.shard_map(local, mesh=mesh, in_specs=in_specs, out_specs=out_specs, check_vma=False)
```

profile of v0, /device:TPU:0, one launch (start us, length us, event | category | flops | bytes accessed | tf_op | source)
XLA Modules:
  0.0 1104.3 jit_solution(12216921466018292153)
XLA Ops:
  14.0 698.9 %while.26 = (s32[]{:T(128)}, f32[768,2304]{1,0:T(8,128)}, f32[768,768]{1,0:T(8,128)}, f32[768,2304]{1,0:T(8,128)}, f32[1152,768]{1,0:T(8,128)}, /*index=5*/f32[2...) while((s32[]{:T(128)}, f32[768,2304]{1,0:T(8,128)}, ...), condition=%wide.region_16.17_spmd.clone.clone.clone, body=%wide.region_0.16_spmd.clone.clone.clone.sunk | while | flops 20481859584 | bytes 894956672 | solution.py:243
  15.2 6.0 all-gather.10
  23.7 27.1 %all-gather.19.cloned.1.call-done = bf16[768,2304]{1,0:T(8,128)(2,1)} async-done(((bf16[192,2304]{1,0:T(8,128)(2,1)}), bf16[768,2304]{1,0:T(8,128)(2,1)}) %all-gather.19.cloned.1.call-update) | async-done | bytes 3538960 | tf_op jit(solution)/shard_map/while/body/eval_jaxpr/all_gather | solution.py:112
  50.8 5.8 copy.94
  56.5 4.2 fusion.183
  73.8 19.9 %all-gather.21.cloned.1.call-done = bf16[2,1024,12,64]{1,3,2,0:T(8,128)(2,1)} async-done(((bf16[2,256,12,64]{1,3,2,0:T(8,128)(2,1)}), bf16[2,1024,12,64]{1,3,2,0:T(8,128)(2,1)}) %all-gather.21.cloned.1.call-update) | async-done | bytes 3145744 | tf_op jit(solution)/shard_map/while/body/eval_jaxpr/all_gather | solution.py:131
  93.6 12.8 %fusion.184 = (f32[2,12,256]{2,1,0:T(8,128)S(1)}, f32[2,12,256,1024]{3,2,1,0:T(8,128)}) fusion(pred[2,1024]{1,0:T(4,128)(4,1)S(1)} %iota_compare_fusion.2, bf16[2,1024,12,64]{1,3,2,0:T(8,128)(2,1)} %all-gather.21.cloned.1.call-done, bf16[2,256,12,32]{1,3,2,0:T(8,128)(2,1)S(1)} %get-tuple-element.666, bf16[2,256,12,32]{1,3,2,0:T(8,128)(2,1)S(1)} %get-tuple-element.667), kind=kOutput, calls=%fused_computation.16.clone.1 | convolution fusion | flops 825747456 | bytes 29124608 | tf_op jit(solution)/shard_map/while/body/eval_jaxpr/sqhd,skhd->shqk/dot_general | solution.py:54
  106.5 11.4 %fusion.185 = f32[2,12,256]{2,1,0:T(8,128)S(1)} fusion(f32[2,12,256]{2,1,0:T(8,128)S(1)} %get-tuple-element.668, f32[2,12,256,1024]{3,2,1,0:T(8,128)} %get-tuple-element.669, pred[2,1024]{1,0:T(4,128)(4,1)S(1)} %iota_compare_fusion.2), kind=kLoop, calls=%fused_computation.11.clone.1 | loop fusion | flops 25159680 | bytes 25217024 | tf_op jit(solution)/shard_map/while/body/eval_jaxpr/reduce_sum | solution.py:137
  117.9 6.8 all-gather.23.cloned.1.call-done
  124.7 12.9 %fusion.186 = bf16[2,256,12,64]{1,3,2,0:T(8,128)(2,1)S(1)} fusion(f32[2,12,256]{2,1,0:T(8,128)S(1)} %fusion.185, f32[2,12,256]{2,1,0:T(8,128)S(1)} %get-tuple-element.668, f32[2,12,256,1024]{3,2,1,0:T(8,128)} %get-tuple-element.669, pred[2,1024]{1,0:T(4,128)(4,1)S(1)} %iota_compare_fusion.2, ...), kind=kOutput, calls=%fused_computation.69.clone.1 | convolution fusion | flops 837156864 | bytes 29149184 | tf_op jit(solution)/shard_map/while/body/eval_jaxpr/shqk,skhd->sqhd/dot_general | solution.py:140
  139.5 4.7 all-gather.25.cloned.1.call-done
  148.9 28.0 %all-gather.27.cloned.1.call-done = bf16[768,2304]{1,0:T(8,128)(2,1)} async-done(((bf16[192,2304]{1,0:T(8,128)(2,1)}), bf16[768,2304]{1,0:T(8,128)(2,1)}) %all-gather.27.cloned.1.call-update) | async-done | bytes 3538960 | tf_op jit(solution)/shard_map/while/body/eval_jaxpr/all_gather | solution.py:114
  177.0 6.3 fusion.189
  183.3 16.4 %all-gather.29.cloned.1.call-done = bf16[1152,768]{1,0:T(8,128)(2,1)} async-done(((bf16[288,768]{1,0:T(8,128)(2,1)}), bf16[1152,768]{1,0:T(8,128)(2,1)}) %all-gather.29.cloned.1.call-update) | async-done | bytes 1769488 | tf_op jit(solution)/shard_map/while/body/eval_jaxpr/all_gather | solution.py:160
  199.8 6.4 fusion.192
  216.1 2.9 reshape.379
  219.0 19.6 %multiply_reduce_fusion.9 = (f32[2,12,256]{2,1,0:T(8,128)}, f32[2,12,256,1024]{3,2,1,0:T(8,128)}) fusion(f32[2,12,256]{2,1,0:T(8,128)} %log_add_fusion.2, f32[2,12,256,1024]{3,2,1,0:T(8,128)} %get-tuple-element.669, pred[2,1024]{1,0:T(4,128)(4,1)S(1)} %iota_compare_fusion.2, bf16[2,1024,1,12,64]{1,4,3,2,0:T(8,128)(2,1)} %all-gather.23.cloned.1.call-done, ...), kind=kOutput, calls=%fused_computation.6.clone.1 | convolution fusion | flops 836757504 | bytes 54315008 | tf_op jit(solution)/shard_map/while/body/eval_jaxpr/sqhd,skhd->shqk/dot_general | solution.py:195
  238.6 16.9 %multiply_convert_fusion.13 = bf16[2,12,256,1024]{3,2,1,0:T(8,128)(2,1)S(1)} fusion(f32[2,12,256,1024]{3,2,1,0:T(8,128)} %get-tuple-element.681, f32[2,12,256]{2,1,0:T(8,128)} %get-tuple-element.682, f32[2,12,256]{2,1,0:T(8,128)} %log_add_fusion.2, f32[2,12,256,1024]{3,2,1,0:T(8,128)} %get-tuple-element.669, pred[2,1024]{1,0:T(4,128)(4,1)S(1)} %iota_compare_fusion.2), kind=kLoop, calls=%fused_computation.5.clone.1 | loop fusion | flops 37748736 | bytes 62965760 | tf_op jit(solution)/shard_map/while/body/eval_jaxpr/convert_element_type | solution.py:199
  255.5 4.6 copy-done
  260.1 3.9 fusion.195
  264.8 14.4 %convert_bitcast_fusion.2 = bf16[2,1024,12,64]{1,3,2,0:T(8,128)(2,1)} fusion(f32[2,12,256]{2,1,0:T(8,128)S(1)} %copy-done.37, f32[2,12,256,1024]{3,2,1,0:T(8,128)} %get-tuple-element.669, pred[2,1024]{1,0:T(4,128)(4,1)S(1)} %iota_compare_fusion.2, bf16[2,256,12,64]{1,0,3,2:T(2,128)(2,1)} %reshape.379), kind=kOutput, calls=%fused_computation.27.clone.1 | convolution fusion | flops 832045056 | bytes 29124608 | tf_op jit(solution)/shard_map/while/body/eval_jaxpr/shqk,sqhd->skhd/dot_general | solution.py:208
  280.8 3.7 multiply_convert_fusion.14
  293.7 5.2 select_add_fusion.8
  299.0 8.6 multiply_bitcast_fusion.2
  309.6 33.2 %reduce-scatter.20.cloned.1.call-done = bf16[2,256,12,64]{1,3,2,0:T(8,128)(2,1)} async-done(((bf16[2,1024,12,64]{1,3,2,0:T(8,128)(2,1)}), bf16[2,256,12,64]{1,3,2,0:T(8,128)(2,1)}) %reduce-scatter.20.cloned.1.call-update) | async-done | bytes 786448 | tf_op jit(solution)/shard_map/while/body/eval_jaxpr/reduce_scatter | solution.py:215
  344.2 2.9 copy.99
  355.1 4.3 select_add_fusion.6
  363.5 5.1 all-gather.10
  371.0 25.4 %all-gather.19.cloned.1.call-done = bf16[768,2304]{1,0:T(8,128)(2,1)} async-done(((bf16[192,2304]{1,0:T(8,128)(2,1)}), bf16[768,2304]{1,0:T(8,128)(2,1)}) %all-gather.19.cloned.1.call-update) | async-done | bytes 3538960 | tf_op jit(solution)/shard_map/while/body/eval_jaxpr/all_gather | solution.py:112
  396.3 5.8 copy.94
  402.1 4.2 fusion.183
  419.5 19.6 %all-gather.21.cloned.1.call-done = bf16[2,1024,12,64]{1,3,2,0:T(8,128)(2,1)} async-done(((bf16[2,256,12,64]{1,3,2,0:T(8,128)(2,1)}), bf16[2,1024,12,64]{1,3,2,0:T(8,128)(2,1)}) %all-gather.21.cloned.1.call-update) | async-done | bytes 3145744 | tf_op jit(solution)/shard_map/while/body/eval_jaxpr/all_gather | solution.py:131
  439.1 12.8 %fusion.184 = (f32[2,12,256]{2,1,0:T(8,128)S(1)}, f32[2,12,256,1024]{3,2,1,0:T(8,128)}) fusion(pred[2,1024]{1,0:T(4,128)(4,1)S(1)} %iota_compare_fusion.2, bf16[2,1024,12,64]{1,3,2,0:T(8,128)(2,1)} %all-gather.21.cloned.1.call-done, bf16[2,256,12,32]{1,3,2,0:T(8,128)(2,1)S(1)} %get-tuple-element.666, bf16[2,256,12,32]{1,3,2,0:T(8,128)(2,1)S(1)} %get-tuple-element.667), kind=kOutput, calls=%fused_computation.16.clone.1 | convolution fusion | flops 825747456 | bytes 29124608 | tf_op jit(solution)/shard_map/while/body/eval_jaxpr/sqhd,skhd->shqk/dot_general | solution.py:54
  451.9 11.4 %fusion.185 = f32[2,12,256]{2,1,0:T(8,128)S(1)} fusion(f32[2,12,256]{2,1,0:T(8,128)S(1)} %get-tuple-element.668, f32[2,12,256,1024]{3,2,1,0:T(8,128)} %get-tuple-element.669, pred[2,1024]{1,0:T(4,128)(4,1)S(1)} %iota_compare_fusion.2), kind=kLoop, calls=%fused_computation.11.clone.1 | loop fusion | flops 25159680 | bytes 25217024 | tf_op jit(solution)/shard_map/while/body/eval_jaxpr/reduce_sum | solution.py:137
  463.4 6.9 all-gather.23.cloned.1.call-done
  470.2 12.6 %fusion.186 = bf16[2,256,12,64]{1,3,2,0:T(8,128)(2,1)S(1)} fusion(f32[2,12,256]{2,1,0:T(8,128)S(1)} %fusion.185, f32[2,12,256]{2,1,0:T(8,128)S(1)} %get-tuple-element.668, f32[2,12,256,1024]{3,2,1,0:T(8,128)} %get-tuple-element.669, pred[2,1024]{1,0:T(4,128)(4,1)S(1)} %iota_compare_fusion.2, ...), kind=kOutput, calls=%fused_computation.69.clone.1 | convolution fusion | flops 837156864 | bytes 29149184 | tf_op jit(solution)/shard_map/while/body/eval_jaxpr/shqk,skhd->sqhd/dot_general | solution.py:140
  484.7 5.0 all-gather.25.cloned.1.call-done
  494.4 28.2 %all-gather.27.cloned.1.call-done = bf16[768,2304]{1,0:T(8,128)(2,1)} async-done(((bf16[192,2304]{1,0:T(8,128)(2,1)}), bf16[768,2304]{1,0:T(8,128)(2,1)}) %all-gather.27.cloned.1.call-update) | async-done | bytes 3538960 | tf_op jit(solution)/shard_map/while/body/eval_jaxpr/all_gather | solution.py:114
  522.6 6.4 fusion.189
  529.0 16.4 %all-gather.29.cloned.1.call-done = bf16[1152,768]{1,0:T(8,128)(2,1)} async-done(((bf16[288,768]{1,0:T(8,128)(2,1)}), bf16[1152,768]{1,0:T(8,128)(2,1)}) %all-gather.29.cloned.1.call-update) | async-done | bytes 1769488 | tf_op jit(solution)/shard_map/while/body/eval_jaxpr/all_gather | solution.py:160
  545.4 6.4 fusion.192
  561.7 2.9 reshape.379
  564.6 19.8 %multiply_reduce_fusion.9 = (f32[2,12,256]{2,1,0:T(8,128)}, f32[2,12,256,1024]{3,2,1,0:T(8,128)}) fusion(f32[2,12,256]{2,1,0:T(8,128)} %log_add_fusion.2, f32[2,12,256,1024]{3,2,1,0:T(8,128)} %get-tuple-element.669, pred[2,1024]{1,0:T(4,128)(4,1)S(1)} %iota_compare_fusion.2, bf16[2,1024,1,12,64]{1,4,3,2,0:T(8,128)(2,1)} %all-gather.23.cloned.1.call-done, ...), kind=kOutput, calls=%fused_computation.6.clone.1 | convolution fusion | flops 836757504 | bytes 54315008 | tf_op jit(solution)/shard_map/while/body/eval_jaxpr/sqhd,skhd->shqk/dot_general | solution.py:195
  584.4 16.9 %multiply_convert_fusion.13 = bf16[2,12,256,1024]{3,2,1,0:T(8,128)(2,1)S(1)} fusion(f32[2,12,256,1024]{3,2,1,0:T(8,128)} %get-tuple-element.681, f32[2,12,256]{2,1,0:T(8,128)} %get-tuple-element.682, f32[2,12,256]{2,1,0:T(8,128)} %log_add_fusion.2, f32[2,12,256,1024]{3,2,1,0:T(8,128)} %get-tuple-element.669, pred[2,1024]{1,0:T(4,128)(4,1)S(1)} %iota_compare_fusion.2), kind=kLoop, calls=%fused_computation.5.clone.1 | loop fusion | flops 37748736 | bytes 62965760 | tf_op jit(solution)/shard_map/while/body/eval_jaxpr/convert_element_type | solution.py:199
  601.3 4.6 copy-done
  605.9 3.9 fusion.195
  610.6 14.3 %convert_bitcast_fusion.2 = bf16[2,1024,12,64]{1,3,2,0:T(8,128)(2,1)} fusion(f32[2,12,256]{2,1,0:T(8,128)S(1)} %copy-done.37, f32[2,12,256,1024]{3,2,1,0:T(8,128)} %get-tuple-element.669, pred[2,1024]{1,0:T(4,128)(4,1)S(1)} %iota_compare_fusion.2, bf16[2,256,12,64]{1,0,3,2:T(2,128)(2,1)} %reshape.379), kind=kOutput, calls=%fused_computation.27.clone.1 | convolution fusion | flops 832045056 | bytes 29124608 | tf_op jit(solution)/shard_map/while/body/eval_jaxpr/shqk,sqhd->skhd/dot_general | solution.py:208
  626.6 3.7 multiply_convert_fusion.14
  639.6 8.4 select_add_fusion.8
  648.0 8.5 multiply_bitcast_fusion.2
  658.5 30.1 %reduce-scatter.20.cloned.1.call-done = bf16[2,256,12,64]{1,3,2,0:T(8,128)(2,1)} async-done(((bf16[2,1024,12,64]{1,3,2,0:T(8,128)(2,1)}), bf16[2,256,12,64]{1,3,2,0:T(8,128)(2,1)}) %reduce-scatter.20.cloned.1.call-update) | async-done | bytes 786448 | tf_op jit(solution)/shard_map/while/body/eval_jaxpr/reduce_scatter | solution.py:215
  700.7 4.3 select_add_fusion.6
  714.5 2.9 convert_element_type.214
  719.0 5.1 convert_element_type.212
  724.2 5.1 convert_element_type.216
  729.5 6.6 reduce-scatter.18.cloned.1.call-done
  736.9 27.8 %reduce-scatter.12.cloned.1.call-done = bf16[192,768]{1,0:T(8,128)(2,1)} async-done(((bf16[768,768]{1,0:T(8,128)(2,1)}), bf16[192,768]{1,0:T(8,128)(2,1)}) %reduce-scatter.12.cloned.1.call-update) | async-done | bytes 294928 | tf_op jit(solution)/shard_map/reduce_scatter | solution.py:249
  764.8 32.5 %reduce-scatter.16.cloned.1.call-done = bf16[288,768]{1,0:T(8,128)(2,1)} async-done(((bf16[1152,768]{1,0:T(8,128)(2,1)}), bf16[288,768]{1,0:T(8,128)(2,1)}) %reduce-scatter.16.cloned.1.call-update) | async-done | bytes 442384 | tf_op jit(solution)/shard_map/reduce_scatter | solution.py:255
  797.3 42.9 %reduce-scatter.10.cloned.1.call-done = bf16[192,2304]{1,0:T(8,128)(2,1)} async-done(((bf16[768,2304]{1,0:T(8,128)(2,1)}), bf16[192,2304]{1,0:T(8,128)(2,1)}) %reduce-scatter.10.cloned.1.call-update) | async-done | bytes 884752 | tf_op jit(solution)/shard_map/reduce_scatter | solution.py:246
  840.2 43.1 %reduce-scatter.14.cloned.1.call-done = bf16[192,2304]{1,0:T(8,128)(2,1)} async-done(((bf16[768,2304]{1,0:T(8,128)(2,1)}), bf16[192,2304]{1,0:T(8,128)(2,1)}) %reduce-scatter.14.cloned.1.call-update) | async-done | bytes 884752 | tf_op jit(solution)/shard_map/reduce_scatter | solution.py:252
  883.2 199.7 %all-reduce.4 = (f32[192,2304]{1,0:T(8,128)}, f32[192,768]{1,0:T(8,128)}, f32[192,2304]{1,0:T(8,128)}, f32[288,768]{1,0:T(8,128)}, f32[2,192]{1,0:T(2,128)S(1)}) all-reduce(bf16[192,2304]{1,0:T(8,128)(2,1)} %reduce-scatter.10.cloned.1.call-done, ...), channel_id=1, replica_groups=mesh['dp'=8,'fsdp'=4] {'dp'}, use_global_device_ids=true, to_apply=%region_18.19 | all-reduce | flops 1253760 | bytes 7522560 | tf_op jit(solution)/shard_map/psum | solution.py:262
  1083.5 3.1 multiply_subtract_fusion.5
  1086.6 3.6 multiply_subtract_fusion.4
  1090.2 6.5 multiply_subtract_fusion.2
  (466 shorter events, 129.7 us)
Async XLA Ops:
  14.3 9.4 copy-start.31
  14.3 9.3 copy-start.63
  14.3 9.3 copy-start.66
  14.3 9.3 copy-start.68
  14.3 36.5 %all-gather.19.cloned.1.call-start = ((), (), s32[]{:S(2)}) async-start(), calls=%async_computation.12 | async-start | bytes 4423680 | tf_op jit(solution)/shard_map/while/body/eval_jaxpr/all_gather | solution.py:112
  15.2 78.4 %all-gather.21.cloned.1.call-start = ((), (), s32[]{:S(2)}) async-start(), calls=%async_computation.13 | async-start | bytes 3932160 | tf_op jit(solution)/shard_map/while/body/eval_jaxpr/all_gather | solution.py:131
  21.6 35.0 %copy-start.50 = (f32[768]{0:T(1024)}, f32[768]{0:T(1024)S(1)}, u32[]{:S(2)}) copy-start(f32[768]{0:T(1024)S(1)} %get-tuple-element.657) | copy-start | bytes 9220 | tf_op jit(solution)/shard_map/while
  23.3 39.6 %copy-start.33 = (f32[256,32]{0,1:T(8,128)}, f32[256,32]{0,1:T(8,128)S(1)}, u32[]{:S(2)}) copy-start(f32[256,32]{0,1:T(8,128)S(1)} %get-tuple-element.662) | copy-start | bytes 98308 | tf_op jit(solution)/shard_map/while
  23.7 32.9 %copy-start.9 = (bf16[1,2,256,768]{3,2,1,0:T(8,128)(2,1)}, bf16[1,2,256,768]{3,2,1,0:T(8,128)(2,1)S(1)}, u32[]{:S(2)}) copy-start(bf16[1,2,256,768]{3,2,1,0:T(8,128)(2,1)S(1)} %fusion.181) | copy-start | bytes 2359300 | tf_op jit(solution)/shard_map/while
  63.4 30.2 %copy-start.14 = (bf16[2,256,12,32]{1,3,2,0:T(8,128)(2,1)}, bf16[2,256,12,32]{1,3,2,0:T(8,128)(2,1)S(1)}, u32[]{:S(2)}) copy-start(bf16[2,256,12,32]{1,3,2,0:T(8,128)(2,1)S(1)} %get-tuple-element.666) | copy-start | bytes 1179652 | tf_op jit(solution)/shard_map/while
  64.5 60.2 %all-gather.23.cloned.1.call-start = ((), (), s32[]{:S(2)}) async-start(), calls=%async_computation.14 | async-start | bytes 3932160 | tf_op jit(solution)/shard_map/while/body/eval_jaxpr/all_gather | solution.py:132
  67.0 77.3 %all-gather.25.cloned.1.call-start = ((), (), s32[]{:S(2)}) async-start(), calls=%async_computation.15 | async-start | bytes 1474560 | tf_op jit(solution)/shard_map/while/body/eval_jaxpr/all_gather | solution.py:113
  67.5 109.5 %all-gather.27.cloned.1.call-start = ((), (), s32[]{:S(2)}) async-start(), calls=%async_computation.16 | async-start | bytes 4423680 | tf_op jit(solution)/shard_map/while/body/eval_jaxpr/all_gather | solution.py:114
  68.1 131.7 %all-gather.29.cloned.1.call-start = ((), (), s32[]{:S(2)}) async-start(), calls=%async_computation.17 | async-start | bytes 2211840 | tf_op jit(solution)/shard_map/while/body/eval_jaxpr/all_gather | solution.py:160
  68.7 238.9 %reduce-scatter.22.cloned.1.call-start = ((), (), s32[]{:S(2)}) async-start(), calls=%async_computation.19 | async-start | bytes 3932160 | tf_op jit(solution)/shard_map/while/body/eval_jaxpr/reduce_scatter | solution.py:212
  106.5 18.3 %copy-start.35 = (f32[2,12,256]{2,1,0:T(8,128)}, f32[2,12,256]{2,1,0:T(8,128)S(1)}, u32[]{:S(2)}) copy-start(f32[2,12,256]{2,1,0:T(8,128)S(1)} %get-tuple-element.668) | copy-start | bytes 73732 | tf_op jit(solution)/shard_map/while
  117.9 19.8 %copy-start.43 = (f32[2,12,256]{2,1,0:T(8,128)}, f32[2,12,256]{2,1,0:T(8,128)S(1)}, u32[]{:S(2)}) copy-start(f32[2,12,256]{2,1,0:T(8,128)S(1)} %fusion.185) | copy-start | bytes 73732 | tf_op jit(solution)/shard_map/while
  238.5 21.5 %copy-start.15 = (bf16[2,256,12,32]{1,3,2,0:T(8,128)(2,1)S(1)}, bf16[2,256,12,32]{1,3,2,0:T(8,128)(2,1)}, u32[]{:S(2)}) copy-start(bf16[2,256,12,32]{1,3,2,0:T(8,128)(2,1)} %copy-done.14) | copy-start | bytes 1179652 | tf_op jit(solution)/shard_map/while
  264.0 78.8 %reduce-scatter.20.cloned.1.call-start = ((), (), s32[]{:S(2)}) async-start(), calls=%async_computation.18 | async-start | bytes 3932160 | tf_op jit(solution)/shard_map/while/body/eval_jaxpr/reduce_scatter | solution.py:215
  344.2 10.8 slice-start
  355.1 7.2 copy-start.29
  355.1 7.2 copy-start.32
  355.1 7.2 copy-start.64
  355.1 7.2 copy-start.67
  355.1 7.2 copy-start.69
  362.5 8.4 copy-start.31
  362.5 8.4 copy-start.63
  362.5 8.4 copy-start.66
  362.5 8.4 copy-start.68
  362.5 33.8 %all-gather.19.cloned.1.call-start = ((), (), s32[]{:S(2)}) async-start(), calls=%async_computation.12 | async-start | bytes 4423680 | tf_op jit(solution)/shard_map/while/body/eval_jaxpr/all_gather | solution.py:112
  363.4 75.7 %all-gather.21.cloned.1.call-start = ((), (), s32[]{:S(2)}) async-start(), calls=%async_computation.13 | async-start | bytes 3932160 | tf_op jit(solution)/shard_map/while/body/eval_jaxpr/all_gather | solution.py:131
  368.8 33.2 %copy-start.50 = (f32[768]{0:T(1024)}, f32[768]{0:T(1024)S(1)}, u32[]{:S(2)}) copy-start(f32[768]{0:T(1024)S(1)} %get-tuple-element.657) | copy-start | bytes 9220 | tf_op jit(solution)/shard_map/while
  370.6 37.8 %copy-start.33 = (f32[256,32]{0,1:T(8,128)}, f32[256,32]{0,1:T(8,128)S(1)}, u32[]{:S(2)}) copy-start(f32[256,32]{0,1:T(8,128)S(1)} %get-tuple-element.662) | copy-start | bytes 98308 | tf_op jit(solution)/shard_map/while
  370.9 31.1 %copy-start.9 = (bf16[1,2,256,768]{3,2,1,0:T(8,128)(2,1)}, bf16[1,2,256,768]{3,2,1,0:T(8,128)(2,1)S(1)}, u32[]{:S(2)}) copy-start(bf16[1,2,256,768]{3,2,1,0:T(8,128)(2,1)S(1)} %fusion.181) | copy-start | bytes 2359300 | tf_op jit(solution)/shard_map/while
  409.0 30.1 %copy-start.14 = (bf16[2,256,12,32]{1,3,2,0:T(8,128)(2,1)}, bf16[2,256,12,32]{1,3,2,0:T(8,128)(2,1)S(1)}, u32[]{:S(2)}) copy-start(bf16[2,256,12,32]{1,3,2,0:T(8,128)(2,1)S(1)} %get-tuple-element.666) | copy-start | bytes 1179652 | tf_op jit(solution)/shard_map/while
  410.0 60.2 %all-gather.23.cloned.1.call-start = ((), (), s32[]{:S(2)}) async-start(), calls=%async_computation.14 | async-start | bytes 3932160 | tf_op jit(solution)/shard_map/while/body/eval_jaxpr/all_gather | solution.py:132
  412.5 77.2 %all-gather.25.cloned.1.call-start = ((), (), s32[]{:S(2)}) async-start(), calls=%async_computation.15 | async-start | bytes 1474560 | tf_op jit(solution)/shard_map/while/body/eval_jaxpr/all_gather | solution.py:113
  413.1 109.6 %all-gather.27.cloned.1.call-start = ((), (), s32[]{:S(2)}) async-start(), calls=%async_computation.16 | async-start | bytes 4423680 | tf_op jit(solution)/shard_map/while/body/eval_jaxpr/all_gather | solution.py:114
  413.8 131.6 %all-gather.29.cloned.1.call-start = ((), (), s32[]{:S(2)}) async-start(), calls=%async_computation.17 | async-start | bytes 2211840 | tf_op jit(solution)/shard_map/while/body/eval_jaxpr/all_gather | solution.py:160
  414.4 242.1 %reduce-scatter.22.cloned.1.call-start = ((), (), s32[]{:S(2)}) async-start(), calls=%async_computation.19 | async-start | bytes 3932160 | tf_op jit(solution)/shard_map/while/body/eval_jaxpr/reduce_scatter | solution.py:212
  451.9 18.3 %copy-start.35 = (f32[2,12,256]{2,1,0:T(8,128)}, f32[2,12,256]{2,1,0:T(8,128)S(1)}, u32[]{:S(2)}) copy-start(f32[2,12,256]{2,1,0:T(8,128)S(1)} %get-tuple-element.668) | copy-start | bytes 73732 | tf_op jit(solution)/shard_map/while
  463.3 19.5 %copy-start.43 = (f32[2,12,256]{2,1,0:T(8,128)}, f32[2,12,256]{2,1,0:T(8,128)S(1)}, u32[]{:S(2)}) copy-start(f32[2,12,256]{2,1,0:T(8,128)S(1)} %fusion.185) | copy-start | bytes 73732 | tf_op jit(solution)/shard_map/while
  584.4 21.5 %copy-start.15 = (bf16[2,256,12,32]{1,3,2,0:T(8,128)(2,1)S(1)}, bf16[2,256,12,32]{1,3,2,0:T(8,128)(2,1)}, u32[]{:S(2)}) copy-start(bf16[2,256,12,32]{1,3,2,0:T(8,128)(2,1)} %copy-done.14) | copy-start | bytes 1179652 | tf_op jit(solution)/shard_map/while
  609.9 78.6 %reduce-scatter.20.cloned.1.call-start = ((), (), s32[]{:S(2)}) async-start(), calls=%async_computation.18 | async-start | bytes 3932160 | tf_op jit(solution)/shard_map/while/body/eval_jaxpr/reduce_scatter | solution.py:215
  639.6 8.4 copy-start.8
  689.9 10.6 slice-start
  700.6 7.2 copy-start.29
  700.7 7.2 copy-start.32
  700.7 7.2 copy-start.64
  700.7 7.2 copy-start.67
  700.7 7.2 copy-start.69
  712.9 23.2 %reduce-scatter.18.cloned.1.call-start = ((), (), s32[]{:S(2)}) async-start(), calls=%async_computation.11 | async-start | bytes 245760
  714.5 50.3 %reduce-scatter.12.cloned.1.call-start = ((), (), s32[]{:S(2)}) async-start(), calls=%async_computation.8 | async-start | bytes 1474560 | tf_op jit(solution)/shard_map/reduce_scatter | solution.py:249
  717.5 79.8 %reduce-scatter.16.cloned.1.call-start = ((), (), s32[]{:S(2)}) async-start(), calls=%async_computation.10 | async-start | bytes 2211840 | tf_op jit(solution)/shard_map/reduce_scatter | solution.py:255
  719.0 121.2 %reduce-scatter.10.cloned.1.call-start = ((), (), s32[]{:S(2)}) async-start(), calls=%async_computation.7 | async-start | bytes 4423680 | tf_op jit(solution)/shard_map/reduce_scatter | solution.py:246
  724.2 159.0 %reduce-scatter.14.cloned.1.call-start = ((), (), s32[]{:S(2)}) async-start(), calls=%async_computation.9 | async-start | bytes 4423680 | tf_op jit(solution)/shard_map/reduce_scatter | solution.py:252
  729.4 357.2 %copy-start.52 = (f32[288,768]{1,0:T(8,128)S(1)}, f32[288,768]{1,0:T(8,128)}, u32[]{:S(2)}) copy-start(f32[288,768]{1,0:T(8,128)} %param.31) | copy-start | bytes 2654212
  729.4 353.5 %copy-start.70 = (f32[2,192]{1,0:T(2,128)S(1)}, f32[2,192]{1,0:T(2,128)}, u32[]{:S(2)}) copy-start(f32[2,192]{1,0:T(2,128)} %param.27) | copy-start | bytes 4612
  729.4 353.5 %copy-start.71 = (f32[2,192]{1,0:T(2,128)S(1)}, f32[2,192]{1,0:T(2,128)}, u32[]{:S(2)}) copy-start(f32[2,192]{1,0:T(2,128)} %param.32) | copy-start | bytes 4612
  729.4 353.5 %copy-start.72 = (f32[2,192]{1,0:T(2,128)S(1)}, f32[2,192]{1,0:T(2,128)}, u32[]{:S(2)}) copy-start(f32[2,192]{1,0:T(2,128)} %param.37) | copy-start | bytes 4612
  729.4 354.1 %copy-start.45 = (f32[192,768]{1,0:T(8,128)S(1)}, f32[192,768]{1,0:T(8,128)}, u32[]{:S(2)}) copy-start(f32[192,768]{1,0:T(8,128)} %param.24) | copy-start | bytes 1769476
  883.2 207.0 %copy-start.49 = (f32[192,2304]{1,0:T(8,128)S(1)}, f32[192,2304]{1,0:T(8,128)}, u32[]{:S(2)}) copy-start(f32[192,2304]{1,0:T(8,128)} %param.28) | copy-start | bytes 5308420
  1083.5 6.7 copy-start.47
  1083.5 6.7 copy-start.48
  (103 other events, 270.8 us)
Sparse Core Ops, SparseCore 0:
  17.3 33.4 all-gather.18
  64.6 28.9 all-gather.20
  95.8 28.9 all-gather.22
  126.7 17.4 all-gather.24
  146.2 30.7 all-gather.26
  179.0 20.7 all-gather.28
  264.2 37.9 reduce-scatter.21
  304.8 37.9 reduce-scatter.19
  365.5 30.7 all-gather.18
  410.1 28.9 all-gather.20
  441.2 28.9 all-gather.22
  472.2 17.4 all-gather.24
  491.8 30.7 all-gather.26
  524.6 20.7 all-gather.28
  610.0 37.9 reduce-scatter.21
  650.6 37.9 reduce-scatter.19
Sparse Core Ops, SparseCore 1:
  716.3 19.7 reduce-scatter.17
  739.1 25.6 reduce-scatter.11
  768.0 29.3 reduce-scatter.15
  799.9 40.2 reduce-scatter.9
  842.9 40.2 reduce-scatter.13
where the time goes:
time: 1110 us; the launch traced here: 1100 us
  waiting for transfers between devices  424 us (38%)
  matrix products  233 us (21%)
  blocking collectives  211 us (19%)
  other arithmetic  118 us (11%)
  local copies, waits for them, and re-layouts  94.6 us (9%)
  between operations  15.9 us (1%)
    psum x1, blocking collectives, local(): lax.psum((shards[0], shards[1], shards[2], shards[3], shards[4]), 'dp')  200 us
    reduce_scatter x2, waiting for transfers between devices, micro_step(): lax.psum_scatter(value_part.astype(jnp.bfloat16), 'fsdp', scatter_dimensi...  63.3 us
    all_gather x2, waiting for transfers between devices, micro_step(): lax.all_gather(expand_copy, 'fsdp', axis=0, tiled=True)  56.2 us
    all_gather x2, waiting for transfers between devices, micro_step(): lax.all_gather(inward_copy, 'fsdp', axis=0, tiled=True)  52.5 us
    while x270, local copies, waits for them, and re-layouts  51.2 us
    reduce_scatter x1, waiting for transfers between devices, local(): lax.psum_scatter(accum[2].astype(jnp.bfloat16), 'fsdp', scatter_dimension...  43.1 us
    reduce_scatter x1, waiting for transfers between devices, local(): lax.psum_scatter(accum[0].astype(jnp.bfloat16), 'fsdp', scatter_dimension...  42.9 us
    all_gather x2, waiting for transfers between devices, micro_step(): lax.all_gather(keys_local, 'fsdp', axis=1, tiled=True)  39.5 us
  transfers between devices with their start and end apart: 21, of which 19 were waited for; matrix products, arithmetic and copies ran while one was open for 19% of the time, Pallas kernels for 0%

commit v1 on v0

v1 whole, which is shorter than its diff:
```python
import functools

import jax
import jax.numpy as jnp
from jax import lax
from jax.experimental import pallas as pl
from jax.experimental.pallas import tpu as pltpu
from jax.sharding import PartitionSpec as P

FF = 1152
HEADS = 12
HDIM = 64
STEP = 10

rope_base = 160000.0
norm_eps = 1e-05
adam_beta = 0.5
adam_eps = 1e-08
weight_decay = 0.01
rates = (0.07, 2.0, 0.07, 0.06, 0.2)
masked_score = -1e30

BF = jnp.bfloat16
F32 = jnp.float32
NN = (((1,), (0,)), ((), ()))
NT = (((1,), (1,)), ((), ()))
TN = (((0,), (0,)), ((), ()))
VMEM_BYTES = 58 << 20
LANES = 128
PAIRS = HEADS * HDIM // LANES


def dot(left, right, dims=NN):
    return lax.dot_general(left, right, dims, preferred_element_type=F32)


def swap_halves(values):
    lane = lax.broadcasted_iota(jnp.int32, (1, LANES), 1)
    former = lax.rem(lane, HDIM) < HDIM // 2
    ahead = pltpu.roll(values, LANES - HDIM // 2, 1)
    behind = pltpu.roll(values, HDIM // 2, 1)
    return jnp.where(former, ahead, behind)


def centre_scale(values):
    center = values - jnp.mean(values, axis=-1, keepdims=True)
    spread = jnp.mean(center * center, axis=-1, keepdims=True)
    inverse = lax.rsqrt(spread + norm_eps)
    return center * inverse, inverse


def norm_back(grad, normed, inverse, gain):
    scaled = grad * gain
    mean_one = jnp.mean(scaled, axis=-1, keepdims=True)
    mean_two = jnp.mean(scaled * normed, axis=-1, keepdims=True)
    return inverse * (scaled - mean_one - normed * mean_two)


def place(scratch, pieces, me, rows):
    for r, piece in enumerate(pieces):
        owner = me ^ r
        scratch[pl.ds(pl.multiple_of(owner * rows, 32), rows), :] = piece[...]


def qkv_kernel(info, x_ref, gain_ref, cos_ref, sin_ref, w0, w1, w2, w3, h_ref, ht_ref, qkv_ref, w_ref):
    @pl.when(pl.program_id(0) == 0)
    def _():
        place(w_ref, (w0, w1, w2, w3), info[0], w0.shape[0])

    normed, unused = centre_scale(x_ref[...].astype(F32))
    hidden = normed * gain_ref[0:1, :]
    low = hidden.astype(BF)
    h_ref[...] = low
    ht_ref[...] = low.astype(F32).T.astype(BF)
    cosine = cos_ref[...]
    sine = sin_ref[...]
    width = low.shape[1]
    for part in range(3):
        joined = dot(low, w_ref[:, part * width : (part + 1) * width])
        if part == 2:
            qkv_ref[:, part * width : (part + 1) * width] = joined.astype(BF)
            continue
        for pair in range(PAIRS):
            block = joined[:, pair * LANES : (pair + 1) * LANES]
            turned = block * cosine + swap_halves(block) * sine
            turned = turned.astype(BF)
            if part == 0:
                turned = turned * jnp.asarray(HDIM**-0.5, BF)
            start = part * width + pair * LANES
            qkv_ref[:, start : start + LANES] = turned


def qkv_call(info, x, gain, cosine, sine, pieces, tile=256):
    rows, width = x.shape
    wide = pieces[0].shape[1]
    total = 4 * pieces[0].shape[0]
    whole = lambda i, s: (0, 0)
    by_row = lambda i, s: (i, 0)
    return pl.pallas_call(
        qkv_kernel,
        grid_spec=pltpu.PrefetchScalarGridSpec(
            num_scalar_prefetch=1,
            grid=(rows // tile,),
            in_specs=[
                pl.BlockSpec((tile, width), by_row),
                pl.BlockSpec((2, width), whole),
                pl.BlockSpec((tile, LANES), by_row),
                pl.BlockSpec((tile, LANES), by_row),
            ]
            + [pl.BlockSpec(pieces[0].shape, whole)] * 4,
            out_specs=[
                pl.BlockSpec((tile, width), by_row),
                pl.BlockSpec((width, tile), lambda i, s: (0, i)),
                pl.BlockSpec((tile, wide), by_row),
                pl.BlockSpec((total, wide), whole),
            ],
        ),
        out_shape=[
            jax.ShapeDtypeStruct((rows, width), BF),
            jax.ShapeDtypeStruct((width, rows), BF),
            jax.ShapeDtypeStruct((rows, wide), BF),
            jax.ShapeDtypeStruct((total, wide), BF),
        ],
        compiler_params=pltpu.CompilerParams(vmem_limit_bytes=VMEM_BYTES),
        name="qkv",
    )(info, x, gain, cosine, sine, *pieces)


def attend_kernel(info, q_ref, k_ref, v_ref, o_ref, r_ref, p_ref, *, tile):
    rows = q_ref.shape[0]
    key_at = lax.broadcasted_iota(jnp.int32, (1, rows), 1)
    bias = jnp.where(key_at < info[1], 0.0, masked_score).astype(F32)
    keys = k_ref[...]
    values = v_ref[...]
    low = lax.broadcasted_iota(jnp.int32, (1, LANES), 1) < HDIM
    one = jnp.ones((), BF)
    zero = jnp.zeros((), BF)
    sides = (jnp.where(low, values, one), jnp.where(low, one, values))
    for step in range(rows // tile):
        at = pl.ds(step * tile, tile)
        queries = q_ref[at, :]
        heads = (jnp.where(low, queries, zero), jnp.where(low, zero, queries))
        outs = []
        for head in range(2):
            scores = dot(heads[head], keys, NT) + bias
            peak = jnp.max(scores, axis=-1, keepdims=True)
            terms = jnp.exp(scores - peak).astype(BF)
            p_ref[head, at, :] = terms
            outs.append(dot(terms, sides[head]))
        mixed = jnp.where(low, outs[0], outs[1])
        total = pltpu.roll(jnp.where(low, outs[1], outs[0]), HDIM, 1)
        inverse = 1.0 / total
        o_ref[at, :] = (mixed * inverse).astype(BF)
        r_ref[at, :] = inverse


def attend_call(info, qkv, tile=512):
    rows = qkv.shape[0]
    width = qkv.shape[1] // 3
    block = (rows, LANES)
    return pl.pallas_call(
        functools.partial(attend_kernel, tile=tile),
        grid_spec=pltpu.PrefetchScalarGridSpec(
            num_scalar_prefetch=1,
            grid=(PAIRS,),
            in_specs=[
                pl.BlockSpec(block, lambda p, s: (0, p)),
                pl.BlockSpec(block, lambda p, s: (0, PAIRS + p)),
                pl.BlockSpec(block, lambda p, s: (0, 2 * PAIRS + p)),
            ],
            out_specs=[
                pl.BlockSpec(block, lambda p, s: (0, p)),
                pl.BlockSpec(block, lambda p, s: (0, p)),
                pl.BlockSpec((2, rows, rows), lambda p, s: (p, 0, 0)),
            ],
        ),
        out_shape=[
            jax.ShapeDtypeStruct((rows, width), BF),
            jax.ShapeDtypeStruct((rows, width), F32),
            jax.ShapeDtypeStruct((HEADS, rows, rows), BF),
        ],
        compiler_params=pltpu.CompilerParams(vmem_limit_bytes=VMEM_BYTES),
        name="attend",
    )(info, qkv, qkv, qkv)


def split_rows(source, me, rows, keep, send):
    for r in range(4):
        owner = me ^ r
        value = source[pl.ds(pl.multiple_of(owner * rows, 32), rows), :].astype(BF)
        target = send if r % 2 else keep
        target[r // 2] = value


def feed_kernel(
    info, x_ref, o_ref, r_ref, cot_ref, gain_ref, a0, a1, a2, a3, d0, d1, d2, d3,
    out_ref, dmid_ref, do_ref, gg_ref, ga_keep, ga_send, gd_keep, gd_send,
    wa, wd, acc_o, acc_i, acc_d, *, tile,
):
    step = pl.program_id(0)
    me = info[0]
    width = x_ref.shape[1]

    @pl.when(step == 0)
    def _():
        place(wa, (a0, a1, a2, a3), me, a0.shape[0])
        place(wd, (d0, d1, d2, d3), me, d0.shape[0])
        acc_o[...] = jnp.zeros_like(acc_o)
        acc_i[...] = jnp.zeros_like(acc_i)
        acc_d[...] = jnp.zeros_like(acc_d)
        gg_ref[...] = jnp.zeros_like(gg_ref)

    gain = gain_ref[1:2, :]
    mixed = o_ref[...]
    middle = x_ref[...].astype(F32) + dot(mixed, wa[:, :width])
    normed, inverse = centre_scale(middle)
    hidden = (normed * gain).astype(BF)
    gate = dot(hidden, wa[:, width : width + FF])
    upward = dot(hidden, wa[:, width + FF :])
    cdf = 0.5 * (1.0 + lax.erf(gate * 0.7071067811865476))
    gelu = gate * cdf
    slope = cdf + gate * (jnp.exp(-0.5 * gate * gate) * 0.3989422804014327)
    state = (gelu * upward).astype(BF)
    row_at = step * tile + lax.broadcasted_iota(jnp.int32, (tile, 1), 0)
    live = row_at < info[1]
    out_ref[...] = jnp.where(live, middle + dot(state, wd[...]), 0.0).astype(BF)
    branch = jnp.where(live, cot_ref[...].astype(F32), 0.0)
    branch_low = branch.astype(BF)
    acc_d[...] += dot(state, branch_low, TN)
    state_grad = dot(branch_low, wd[...], NT)
    gate_grad = (state_grad * upward * slope).astype(BF)
    up_grad = (state_grad * gelu).astype(BF)
    acc_i[:, :FF] += dot(hidden, gate_grad, TN)
    acc_i[:, FF:] += dot(hidden, up_grad, TN)
    hidden_grad = dot(gate_grad, wa[:, width : width + FF], NT) + dot(up_grad, wa[:, width + FF :], NT)
    gg_ref[...] += jnp.sum(hidden_grad * normed, axis=0, keepdims=True)
    middle_grad = branch + norm_back(hidden_grad, normed, inverse, gain)
    dmid_ref[...] = middle_grad
    mixer = middle_grad.astype(BF)
    acc_o[...] += dot(mixed, mixer, TN)
    do_ref[...] = (dot(mixer, wa[:, :width], NT) * r_ref[...]).astype(BF)

    @pl.when(step == pl.num_programs(0) - 1)
    def _():
        rows = a0.shape[0]
        for r in range(4):
            at = pl.ds(pl.multiple_of((me ^ r) * rows, 32), rows)
            target = ga_send if r % 2 else ga_keep
            target[r // 2, :, :width] = acc_o[at, :].astype(BF)
            target[r // 2, :, width:] = acc_i[at, :].astype(BF)
        split_rows(acc_d, me, d0.shape[0], gd_keep, gd_send)


def feed_call(info, x, mixed, inverse, cot, gain, a_pieces, d_pieces, tile=256):
    rows, width = x.shape
    ra, ca = a_pieces[0].shape
    rd, cd = d_pieces[0].shape
    whole = lambda i, s: (0, 0)
    cube = lambda i, s: (0, 0, 0)
    by_row = lambda i, s: (i, 0)
    block = pl.BlockSpec((tile, width), by_row)
    return pl.pallas_call(
        functools.partial(feed_kernel, tile=tile),
        grid_spec=pltpu.PrefetchScalarGridSpec(
            num_scalar_prefetch=1,
            grid=(rows // tile,),
            in_specs=[block, block, block, block, pl.BlockSpec((2, width), whole)]
            + [pl.BlockSpec((ra, ca), whole)] * 4
            + [pl.BlockSpec((rd, cd), whole)] * 4,
            out_specs=[block, block, block, pl.BlockSpec((1, width), whole)]
            + [pl.BlockSpec((2, ra, ca), cube)] * 2
            + [pl.BlockSpec((2, rd, cd), cube)] * 2,
            scratch_shapes=[
                pltpu.VMEM((4 * ra, ca), BF),
                pltpu.VMEM((4 * rd, cd), BF),
                pltpu.VMEM((width, width), F32),
                pltpu.VMEM((width, 2 * FF), F32),
                pltpu.VMEM((FF, width), F32),
            ],
        ),
        out_shape=[
            jax.ShapeDtypeStruct((rows, width), BF),
            jax.ShapeDtypeStruct((rows, width), F32),
            jax.ShapeDtypeStruct((rows, width), BF),
            jax.ShapeDtypeStruct((1, width), F32),
        ]
        + [jax.ShapeDtypeStruct((2, ra, ca), BF)] * 2
        + [jax.ShapeDtypeStruct((2, rd, cd), BF)] * 2,
        compiler_params=pltpu.CompilerParams(vmem_limit_bytes=VMEM_BYTES),
        name="feed",
    )(info, x, mixed, inverse, cot, gain, *a_pieces, *d_pieces)


def back_kernel(
    info, q_ref, k_ref, v_ref, o_ref, do_ref, p_ref, cos_ref, sin_ref, ht_ref, wq_ref, wk_ref, wv_ref, *rest,
    tile, first, last,
):
    rest = list(rest)
    if not first:
        carry_ref = rest.pop(0)
    if last:
        x_ref, dmid_ref, gain_ref = rest[:3]
        rest = rest[3:]
    keep_ref, send_ref = rest[:2]
    rest = rest[2:]
    if last:
        dx_ref, gg_ref, acc = rest
    else:
        (acc,) = rest
    step = pl.program_id(0)

    @pl.when(step == 0)
    def _():
        if first:
            acc[...] = jnp.zeros_like(acc)
        else:
            acc[...] = carry_ref[...]

    rows = q_ref.shape[0]
    low = lax.broadcasted_iota(jnp.int32, (1, LANES), 1) < HDIM
    zero = jnp.zeros((), BF)
    keys = k_ref[...]
    values = v_ref[...]
    key_heads = (jnp.where(low, keys, zero), jnp.where(low, zero, keys))
    key_grads = [None, None]
    value_grads = [None, None]
    query_grads = []
    for part in range(rows // tile):
        at = pl.ds(part * tile, tile)
        queries = q_ref[at, :]
        grads = do_ref[at, :]
        wide = grads.astype(F32)
        inner = wide * o_ref[at, :].astype(F32)
        grad_heads = (jnp.where(low, grads, zero), jnp.where(low, zero, grads))
        queries_t = queries.astype(F32).T.astype(BF)
        grads_t = wide.T.astype(BF)
        query_grad = None
        for head in range(2):
            mine = low if head == 0 else jnp.logical_not(low)
            lanes = slice(head * HDIM, (head + 1) * HDIM)
            row_inner = jnp.sum(jnp.where(mine, inner, 0.0), axis=-1, keepdims=True)
            term_grad = dot(grad_heads[head], values, NT)
            terms = p_ref[head, at, :]
            score_grad = (terms.astype(F32) * (term_grad - row_inner)).astype(BF)
            partial = dot(score_grad, key_heads[head])
            query_grad = partial if query_grad is None else query_grad + partial
            for grad_list, left, right in (
                (key_grads, queries_t, score_grad),
                (value_grads, grads_t, terms),
            ):
                value = dot(left[lanes], right)
                grad_list[head] = value if grad_list[head] is None else grad_list[head] + value
        query_grads.append(query_grad)
    cosine = cos_ref[...]
    sine = sin_ref[...]
    query_grad = jnp.concatenate(query_grads, axis=0) * (HDIM**-0.5)
    key_grad = jnp.concatenate(key_grads, axis=0).T
    value_grad = jnp.concatenate(value_grads, axis=0).T
    joined = jnp.concatenate(
        [
            (query_grad * cosine - swap_halves(query_grad) * sine).astype(BF),
            (key_grad * cosine - swap_halves(key_grad) * sine).astype(BF),
            value_grad.astype(BF),
        ],
        axis=1,
    )
    weight = jnp.concatenate([wq_ref[...], wk_ref[...], wv_ref[...]], axis=1)
    acc[...] += dot(joined, weight, NT)
    weight_grad = dot(ht_ref[...], joined).astype(BF)
    share = keep_ref.shape[1]
    me = info[0]
    for owner in range(4):
        rel = me ^ owner
        value = weight_grad[owner * share : (owner + 1) * share, :]
        for target, odd in ((keep_ref, 0), (send_ref, 1)):

            @pl.when(rel % 2 == odd)
            def _():
                target[rel // 2] = value

    if last:

        @pl.when(step == pl.num_programs(0) - 1)
        def _():
            normed, inverse = centre_scale(x_ref[...].astype(F32))
            hidden_grad = acc[...]
            gg_ref[...] = jnp.sum(hidden_grad * normed, axis=0, keepdims=True)
            back = norm_back(hidden_grad, normed, inverse, gain_ref[0:1, :])
            dx_ref[...] = (dmid_ref[...] + back).astype(BF)


def back_call(info, qkv, mixed, grads, terms, cosine, sine, hidden_t, weight, start, count, carry, tail, tile=512):
    rows, width = mixed.shape
    last = tail is not None
    first = carry is None
    block = (rows, LANES)
    whole = lambda p, s: (0, 0)

    def column(offset):
        return lambda p, s: (0, offset + start + p)

    in_specs = [
        pl.BlockSpec(block, column(0)),
        pl.BlockSpec(block, column(PAIRS)),
        pl.BlockSpec(block, column(2 * PAIRS)),
        pl.BlockSpec(block, column(0)),
        pl.BlockSpec(block, column(0)),
        pl.BlockSpec((2, rows, rows), lambda p, s: (start + p, 0, 0)),
        pl.BlockSpec(block, whole),
        pl.BlockSpec(block, whole),
        pl.BlockSpec((width, rows), whole),
        pl.BlockSpec((width, LANES), column(0)),
        pl.BlockSpec((width, LANES), column(PAIRS)),
        pl.BlockSpec((width, LANES), column(2 * PAIRS)),
    ]
    operands = [qkv, qkv, qkv, mixed, grads, terms, cosine, sine, hidden_t, weight, weight, weight]
    if not first:
        in_specs.append(pl.BlockSpec((rows, width), whole))
        operands.append(carry)
    if last:
        in_specs += [
            pl.BlockSpec((rows, width), whole),
            pl.BlockSpec((rows, width), whole),
            pl.BlockSpec((2, width), whole),
        ]
        operands += list(tail)
    share = width // 4
    piece = (2, share, 3 * LANES)
    out_specs = [pl.BlockSpec(piece, lambda p, s: (0, 0, p))] * 2
    out_shape = [jax.ShapeDtypeStruct((2, share, 3 * LANES * count), BF)] * 2
    scratch = []
    if last:
        out_specs += [pl.BlockSpec((rows, width), whole), pl.BlockSpec((1, width), whole)]
        out_shape += [jax.ShapeDtypeStruct((rows, width), BF), jax.ShapeDtypeStruct((1, width), F32)]
        scratch = [pltpu.VMEM((rows, width), F32)]
    else:
        out_specs.append(pl.BlockSpec((rows, width), whole))
        out_shape.append(jax.ShapeDtypeStruct((rows, width), F32))
    return pl.pallas_call(
        functools.partial(back_kernel, tile=tile, first=first, last=last),
        grid_spec=pltpu.PrefetchScalarGridSpec(
            num_scalar_prefetch=1,
            grid=(count,),
            in_specs=in_specs,
            out_specs=out_specs,
            scratch_shapes=scratch,
        ),
        out_shape=out_shape,
        compiler_params=pltpu.CompilerParams(vmem_limit_bytes=VMEM_BYTES),
        name="back",
    )(info, *operands)


def adam_update(master, gradient, moment_one, moment_two, step_rate, decay_rate):
    first_new = adam_beta * moment_one + (1.0 - adam_beta) * gradient
    second_new = adam_beta * moment_two + (1.0 - adam_beta) * gradient * gradient
    correction = 1.0 - adam_beta**STEP
    direction = first_new / correction / (jnp.sqrt(second_new / correction) + adam_eps)
    renewed = master - step_rate * (direction + decay_rate * master)
    return (renewed, first_new, second_new)


def tables(seq_total):
    half_dim = HDIM // 2
    exponent = jnp.arange(half_dim, dtype=jnp.float32) * (2.0 / HDIM)
    inverse = jnp.power(jnp.float32(rope_base), -exponent)
    angles = jnp.arange(seq_total, dtype=jnp.float32)[:, None] * inverse[None, :]
    cosine = jnp.cos(angles)
    sine = jnp.sin(angles)
    return jnp.tile(cosine, (1, 4)), jnp.concatenate([-sine, sine, -sine, sine], axis=1)


CORE = [(0, 1), (1, 0), (2, 3), (3, 2)]
CROSS = [(0, 2), (1, 3), (2, 0), (3, 1)]


def gather_pieces(shard):
    near = lax.ppermute(shard, "fsdp", CORE)
    far = lax.ppermute(shard, "fsdp", CROSS)
    return shard, near, far, lax.ppermute(far, "fsdp", CORE)


def add_low(left, right):
    return (left.astype(F32) + right.astype(F32)).astype(BF)


def reduce_pieces(keep, send):
    total = add_low(keep, lax.ppermute(send, "fsdp", CORE))
    return add_low(total[0], lax.ppermute(total[1], "fsdp", CROSS))


def local(
    tokens, cotangent, lengths,
    inward_weight, outward_weight, expand_weight, shrink_weight, gain_weight,
    inward_first, outward_first, expand_first, shrink_first, gain_first,
    inward_second, outward_second, expand_second, shrink_second, gain_second,
):
    micro_count, group_size, local_len, width = tokens.shape
    fsdp = lax.axis_size("fsdp")
    assert fsdp == 4 and micro_count * group_size == fsdp
    seq_total = local_len * fsdp
    me = lax.axis_index("fsdp")
    info = jnp.stack([me.astype(jnp.int32), lengths.reshape(fsdp)[me]])

    def to_sequence(array):
        array = array.reshape(fsdp, local_len, width)
        return lax.all_to_all(array, "fsdp", 0, 0).reshape(seq_total, width)

    def to_positions(array):
        array = array.reshape(fsdp, local_len, width)
        return lax.all_to_all(array, "fsdp", 0, 0).reshape(micro_count, group_size, local_len, width)

    inward_pieces = gather_pieces(inward_weight.astype(BF))
    x = to_sequence(tokens)
    gain = lax.all_gather(gain_weight.astype(BF), "fsdp", axis=1, tiled=True).astype(F32)
    a_pieces = gather_pieces(jnp.concatenate([outward_weight.astype(BF), expand_weight.astype(BF)], axis=1))
    d_pieces = gather_pieces(shrink_weight.astype(BF))
    cot = to_sequence(cotangent)
    cosine, sine = tables(seq_total)

    hidden, hidden_t, qkv, weight = qkv_call(info, x, gain, cosine, sine, inward_pieces)
    mixed, inverse, terms = attend_call(info, qkv)
    out, middle_grad, grads, gain_two, ga_keep, ga_send, gd_keep, gd_send = feed_call(
        info, x, mixed, inverse, cot, gain, a_pieces, d_pieces
    )
    block_out = to_positions(out)
    grad_a = reduce_pieces(ga_keep, ga_send)
    grad_d = reduce_pieces(gd_keep, gd_send)
    grad_a, grad_d = lax.psum((grad_a, grad_d), "dp")

    carry = None
    chunks = []
    calls = 3
    for call in range(calls):
        tail = (x, middle_grad, gain) if call == calls - 1 else None
        count = PAIRS // calls
        outs = back_call(
            info, qkv, mixed, grads, terms, cosine, sine, hidden_t, weight, call * count, count, carry, tail
        )
        keep, send, carry = outs[:3]
        chunks.append(reduce_pieces(keep, send))
    input_low, gain_one = outs[2:]
    input_grad = to_positions(input_low).astype(F32)
    grad_w = lax.psum(tuple(chunks), "dp")
    share = inward_weight.shape[0]
    grad_w = jnp.concatenate(grad_w, axis=1).astype(F32)
    grad_w = grad_w.reshape(share, PAIRS, 3, LANES).transpose(0, 2, 1, 3).reshape(share, 3 * width)
    gain_grad = jnp.concatenate([gain_one, gain_two], axis=0)
    gain_grad = lax.psum(gain_grad, ("dp", "fsdp"))
    gain_grad = lax.dynamic_slice(gain_grad, (0, me * share), (2, share))
    grad_a = grad_a.astype(F32)
    grad_o = grad_a[:, :width]
    grad_i = grad_a[:, width:]
    grad_d = grad_d.astype(F32)

    results = [block_out, input_grad]
    results += adam_update(inward_weight, grad_w, inward_first, inward_second, rates[0], weight_decay)
    results += adam_update(outward_weight, grad_o, outward_first, outward_second, rates[1], weight_decay)
    results += adam_update(expand_weight, grad_i, expand_first, expand_second, rates[2], weight_decay)
    results += adam_update(shrink_weight, grad_d, shrink_first, shrink_second, rates[3], weight_decay)
    results += adam_update(gain_weight, gain_grad, gain_first, gain_second, rates[4], 0.0)
    return tuple(results)


def solution(mesh):
    split = P(None, "dp", "fsdp", None)
    rows = P("fsdp", None)
    columns = P(None, "fsdp")
    kinds = (rows, rows, rows, rows, columns)
    in_specs = (split, split, P(None, "dp")) + kinds * 3
    out_specs = (split, split) + (rows,) * 12 + (columns,) * 3
    return jax.shard_map(local, mesh=mesh, in_specs=in_specs, out_specs=out_specs, check_vma=False)
```

time: 1110 us -> 470 us (0.42)
  waiting for transfers between devices: 424 us -> 132 us
  matrix products: 233 us -> 0 us
  Pallas kernels: 0 us -> 138 us
  blocking collectives: 211 us -> 105 us
  other arithmetic: 118 us -> 35.5 us
  local copies, waits for them, and re-layouts: 94.6 us -> 15.1 us
  starting transfers between devices: 0.89 us -> 21.8 us
    dot_general x36 -> x0, matrix products: 233 us -> none  [the longest x2 39.4 us: micro_step(): jnp.einsum('sqhd,skhd->shqk', mixed_grad, values_all, preferred_element_t...]
    reduce_scatter x8 -> x0, waiting for transfers between devices: 210 us -> none  [the longest x2 63.3 us: micro_step(): lax.psum_scatter(value_part.astype(jnp.bfloat16), 'fsdp', scatter_dimensi...]
    all_gather x12 -> x0, waiting for transfers between devices: 204 us -> none  [the longest x2 56.2 us: micro_step(): lax.all_gather(expand_copy, 'fsdp', axis=0, tiled=True)]
    psum x1, blocking collectives: 200 us -> 55.7 us  [local(): gain_grad = lax.psum(gain_grad, ('dp', 'fsdp'))]
    pallas_call x0 -> x6, Pallas kernels: none -> 138 us  [the longest x3 64.7 us: back_call(): pl.pallas_call(functools.partial(back_kernel, tile=tile, first=first, las...]
    ppermute x0 -> x19, waiting for transfers between devices: none -> 81.1 us  [the longest x5 41.7 us: reduce_pieces(): return add_low(total[0], lax.ppermute(total[1], 'fsdp', CROSS))]
    while x270 -> x0, local copies, waits for them, and re-layouts: 51.2 us -> none
    convert_element_type x25 -> x17, other arithmetic: 63.1 us -> 14.7 us  [the longest x10 8.39 us: add_low(): return (left.astype(F32) + right.astype(F32)).astype(BF)]
  transfers between devices with their start and end apart: 21 -> 23, of which waited for: 19 -> 9; matrix products, arithmetic and copies ran while one was open for 19% -> 6% of each run, Pallas kernels for 0% -> 17%
where the time goes in v1:
time: 470 us; the launch traced here: 462 us
  Pallas kernels  138 us (29%)
  waiting for transfers between devices  132 us (28%)
  blocking collectives  105 us (22%)
  other arithmetic  35.5 us (8%)
  starting transfers between devices  21.8 us (5%)
  local copies, waits for them, and re-layouts  15.1 us (3%)
  between operations  14.7 us (3%)
    pallas_call x3, Pallas kernels, back_call(): pl.pallas_call(functools.partial(back_kernel, tile=tile, first=first, las...  64.7 us
    psum x1, blocking collectives, local(): gain_grad = lax.psum(gain_grad, ('dp', 'fsdp'))  55.7 us
    ppermute x5, waiting for transfers between devices, reduce_pieces(): return add_low(total[0], lax.ppermute(total[1], 'fsdp', CROSS))  41.7 us
    ppermute x3, waiting for transfers between devices, gather_pieces(): far = lax.ppermute(shard, 'fsdp', CROSS)  38.6 us
    pallas_call x1, Pallas kernels, feed_call(): pl.pallas_call(functools.partial(feed_kernel, tile=tile), grid_spec=pltpu...  37.8 us
    psum x1, waiting for transfers between devices, local(): grad_w = lax.psum(tuple(chunks), 'dp')  36.5 us
    all_gather x1, blocking collectives, local(): lax.all_gather(gain_weight.astype(BF), 'fsdp', axis=1, tiled=True)  26.3 us
    pallas_call x1, Pallas kernels, attend_call(): pl.pallas_call(functools.partial(attend_kernel, tile=tile), grid_spec=plt...  25.1 us
  transfers between devices with their start and end apart: 23, of which 9 were waited for; matrix products, arithmetic and copies ran while one was open for 6% of the time, Pallas kernels for 17%

profile of v1, /device:TPU:0, one launch (start us, length us, event | category | flops | bytes accessed | tf_op | source)
XLA Modules:
  0.0 462.0 jit_solution(5772634527624622014)
XLA Ops:
  7.2 4.4 all-to-all-start
  11.6 1.1 convert_element_type.140
  12.8 1.1 pad_maximum_fusion.a0
  13.9 2.3 collective-permute-start.4
  16.2 1.0 convert_element_type.139.w0
  17.2 0.7 collective-permute-start.1
  18.0 0.5 collective-permute-start.3
  18.5 13.9 %all-to-all-done = bf16[4,256,768]{2,1,0:T(8,128)(2,1)S(1)} async-done(((bf16[4,256,768]{2,1,0:T(8,128)(2,1)}), bf16[4,256,768]{2,1,0:T(8,128)(2,1)S(1)}, u32[]{:S(2)}, u32[]{:S(2)}) %all-to-all-start) | async-done | bytes 1572896 | tf_op jit(solution)/shard_map/all_to_all | solution.py:507
  32.4 3.7 all-to-all-start.1
  36.2 21.6 %collective-permute-done.4.a2 = bf16[192,3072]{1,0:T(8,128)(2,1)} collective-permute-done((bf16[192,3072]{1,0:T(8,128)(2,1)}, bf16[192,3072]{1,0:T(8,128)(2,1)}, u32[]{:S(2)}, u32[]{:S(2)}) %collective-permute-start.4) | collective-permute-done | bytes 1179680 | tf_op jit(solution)/shard_map/ppermute | solution.py:479
  57.8 2.0 convert_element_type.142.d0
  59.8 17.0 %collective-permute-done.1.w2 = bf16[192,2304]{1,0:T(8,128)(2,1)} collective-permute-done((bf16[192,2304]{1,0:T(8,128)(2,1)}, bf16[192,2304]{1,0:T(8,128)(2,1)}, u32[]{:S(2)}, u32[]{:S(2)}) %collective-permute-start.1) | collective-permute-done | bytes 884768 | tf_op jit(solution)/shard_map/ppermute | solution.py:479
  76.9 26.3 %all-gather = bf16[4,192,2]{1,2,0:T(2,128)(2,1)S(1)} all-gather(bf16[1,192,2]{1,2,0:T(2,128)(2,1)S(1)} %convert_bitcast_fusion.1), channel_id=1, replica_groups=mesh['dp'=8,'fsdp'=4] {'fsdp'}, dimensions={0}, use_global_device_ids=true | all-gather | bytes 3840 | tf_op jit(solution)/shard_map/all_gather | solution.py:515
  103.2 0.7 reshape.132
  103.9 0.4 collective-permute-start.6
  104.5 2.0 fusion.11
  106.6 1.0 copy.54.cos_ref
  107.6 0.6 dynamic_slice.6
  108.2 1.2 pad_add_fusion.info
  109.4 1.3 pad_maximum_fusion.1.sin_ref
  110.7 10.5 %qkv.1 = (bf16[1024,768]{1,0:T(8,128)(2,1)}, bf16[768,1024]{1,0:T(8,128)(2,1)}, bf16[1024,2304]{1,0:T(8,128)(2,1)}, bf16[768,2304]{1,0:T(8,128)(2,1)}) custom-call(s32[2]{0:T(128)} %pad_add_fusion.info, bf16[1024,768]{1,0:T(8,128)(2,1)} %bitcast.55, f32[2,768]{1,0:T(2,128)} %bitcast.65, f32[1024,128]{1,0:T(8,128)} %copy.54.cos_ref, ...), custom_call_target="tpu_custom_call" | custom-call | tf_op jit(solution)/shard_map/qkv/pallas_call | solution.py:99
  121.3 25.1 %attend.1 = (bf16[1024,768]{1,0:T(8,128)(2,1)}, f32[1024,768]{1,0:T(8,128)}, bf16[12,1024,1024]{2,1,0:T(8,128)(2,1)}) custom-call(s32[2]{0:T(128)} %pad_add_fusion.info, bf16[1024,2304]{1,0:T(8,128)(2,1)} %get-tuple-element.41.q_ref.k_ref.v_ref, bf16[1024,2304]{1,0:T(8,128)(2,1)} %get-tuple-element.41.q_ref.k_ref.v_ref, ...), custom_call_target="tpu_custom_call" | custom-call | tf_op jit(solution)/shard_map/attend/pallas_call | solution.py:161
  146.5 1.1 copy-done.6
  147.6 37.8 %feed.1 = (bf16[1024,768]{1,0:T(8,128)(2,1)}, f32[1024,768]{1,0:T(8,128)}, bf16[1024,768]{1,0:T(8,128)(2,1)}, f32[1,768]{1,0:T(1,128)}, bf16[2,192,3072]{2,1,0:T...) custom-call(s32[2]{0:T(128)} %pad_add_fusion.info, ...), custom_call_target="tpu_custom_call" | custom-call | tf_op jit(solution)/shard_map/feed/pallas_call | solution.py:262
  185.4 20.1 %back.3 = (bf16[2,192,768]{2,1,0:T(8,128)(2,1)}, bf16[2,192,768]{2,1,0:T(8,128)(2,1)}, f32[1024,768]{1,0:T(8,128)}) custom-call(s32[2]{0:T(128)} %pad_add_fusion.info, bf16[1024,2304]{1,0:T(8,128)(2,1)} %get-tuple-element.41.q_ref.k_ref.v_ref, bf16[1024,2304]{1,0:T(8,128)(2,1)} %get-tuple-element.41.q_ref.k_ref.v_ref, ...), custom_call_target="tpu_custom_call" | custom-call | tf_op jit(solution)/shard_map/back/pallas_call | solution.py:439
  205.4 0.4 collective-permute-start.9
  206.0 20.6 %back.4 = (bf16[2,192,768]{2,1,0:T(8,128)(2,1)}, bf16[2,192,768]{2,1,0:T(8,128)(2,1)}, f32[1024,768]{1,0:T(8,128)}) custom-call(s32[2]{0:T(128)} %pad_add_fusion.info, bf16[1024,2304]{1,0:T(8,128)(2,1)} %get-tuple-element.41.q_ref.k_ref.v_ref, bf16[1024,2304]{1,0:T(8,128)(2,1)} %get-tuple-element.41.q_ref.k_ref.v_ref, ...), custom_call_target="tpu_custom_call" | custom-call | tf_op jit(solution)/shard_map/back/pallas_call | solution.py:439
  226.6 24.0 %back.5 = (bf16[2,192,768]{2,1,0:T(8,128)(2,1)}, bf16[2,192,768]{2,1,0:T(8,128)(2,1)}, bf16[1024,768]{1,0:T(8,128)(2,1)}, f32[1,768]{1,0:T(1,128)}) custom-call(s32[2]{0:T(128)} %pad_add_fusion.info, bf16[1024,2304]{1,0:T(8,128)(2,1)} %get-tuple-element.41.q_ref.k_ref.v_ref, bf16[1024,2304]{1,0:T(8,128)(2,1)} %get-tuple-element.41.q_ref.k_ref.v_ref, ...), custom_call_target="tpu_custom_call" | custom-call | tf_op jit(solution)/shard_map/back/pallas_call | solution.py:439
  250.7 0.4 collective-permute-start.13
  251.8 0.4 collective-permute-start.10
  252.2 0.7 collective-permute-done.13
  253.1 0.7 slice_bitcast_fusion.4
  253.9 0.9 collective-permute-start.14
  255.0 0.7 slice_bitcast_fusion.6
  255.8 1.0 collective-permute-start.12
  257.0 0.9 add_convert_fusion
  257.9 1.1 slice_bitcast_fusion
  259.0 1.0 collective-permute-start.16
  260.0 0.8 slice_bitcast_fusion.2
  260.8 1.0 collective-permute-start.18
  261.9 0.9 concatenate.21
  262.8 5.3 %collective-permute-done.14 = bf16[192,768]{1,0:T(8,128)(2,1)} collective-permute-done((bf16[192,768]{1,0:T(8,128)(2,1)}, bf16[192,768]{1,0:T(8,128)(2,1)}, u32[]{:S(2)}, u32[]{:S(2)}) %collective-permute-start.14) | collective-permute-done | bytes 294944 | tf_op jit(solution)/shard_map/ppermute | solution.py:489
  268.1 1.1 fusion.6
  269.3 0.9 concatenate.23
  270.1 4.3 collective-permute-done.12
  274.4 1.1 fusion.7
  275.6 0.9 concatenate.22
  276.4 32.0 %collective-permute-done.18 = bf16[288,768]{1,0:T(8,128)(2,1)} collective-permute-done((bf16[288,768]{1,0:T(8,128)(2,1)}, bf16[288,768]{1,0:T(8,128)(2,1)}, u32[]{:S(2)}, u32[]{:S(2)}) %collective-permute-start.18) | collective-permute-done | bytes 442400 | tf_op jit(solution)/shard_map/ppermute | solution.py:489
  308.4 1.9 fusion.4
  310.3 2.7 fusion
  313.0 1.4 copy-done.16
  314.4 23.3 %all_to_all.20 = bf16[4,256,768]{2,1,0:T(8,128)(2,1)} all-to-all(bf16[4,256,768]{2,1,0:T(8,128)(2,1)S(1)} %bitcast.64), channel_id=1, replica_groups=mesh['dp'=8,'fsdp'=4] {'fsdp'}, dimensions={0} | all-to-all | bytes 3145728 | tf_op jit(solution)/shard_map/all_to_all | solution.py:511
  337.7 3.7 all-to-all-start.3
  341.4 55.7 %psum.47 = f32[2,768]{1,0:T(2,128)S(1)} all-reduce(f32[2,768]{1,0:T(2,128)S(1)} %pad_maximum_fusion.2), channel_id=1, replica_groups=mesh['dp'=8,'fsdp'=4] {'dp','fsdp'}, use_global_device_ids=true, to_apply=%region_5.0 | all-reduce | flops 1536 | bytes 12288 | tf_op jit(solution)/shard_map/psum | solution.py:549
  397.1 0.7 multiply_subtract_fusion.4
  397.8 1.9 convert.8
  399.8 36.5 %all-reduce.3.cloned.1.call-done = (bf16[192,2,3,128]{3,2,1,0:T(4,128)(2,1)}, bf16[192,2,3,128]{3,2,1,0:T(4,128)(2,1)}, bf16[192,2,3,128]{3,2,1,0:T(4,128)(2,1)}...) async-done(((bf16[192,2,3,128]{3,2,1,0:T(4,128)(2,1)}, bf16[192,2,3,128]{3,2,1,0:T(4,128)(2,1)}, bf16[192,2,3,128]{3,2,1,0:T(4,128)(2,1)}, bf16[192,3072]{1,0:T(8,128)(2,1)}, ...) | async-done | bytes 2506768 | tf_op jit(solution)/shard_map/psum | solution.py:544
  436.2 2.0 convert_bitcast_fusion
  438.5 1.6 reshape.126
  440.4 0.8 copy-done.12
  441.2 2.9 multiply_subtract_fusion.3
  444.2 3.2 multiply_subtract_fusion.2
  447.5 6.3 %multiply_subtract_fusion = (f32[192,2304]{1,0:T(8,128)}, f32[192,2304]{1,0:T(8,128)}, f32[192,2304]{1,0:T(8,128)}, f32[192,2304]{1,0:T(8,128)}, f32[192,2304]{1,0:T(8,128)}, /*index=5*/f32[192,2304]{1,0:T(8,128)}) fusion(f32[192,2304]{1,0:T(8,128)S(1)} %copy-done.4, f32[192,3072]{1,0:T(8,128)S(1)} %convert_element_type.173, f32[192,2304]{1,0:T(8,128)S(1)} %copy-done.13, ...), kind=kLoop, calls=%fused_computation.11 | loop fusion | flops 12386304 | bytes 24772608 | tf_op jit(solution)/shard_map/sub | solution.py:459
  453.8 1.1 copy.66
  (102 shorter events, 2.9 us)
Async XLA Ops:
  7.2 5.5 %copy-start.3 = (f32[192,2304]{1,0:T(8,128)S(1)}, f32[192,2304]{1,0:T(8,128)}, u32[]{:S(2)}) copy-start(f32[192,2304]{1,0:T(8,128)} %param.23) | copy-start | bytes 5308420
  7.2 25.2 %all-to-all-start = ((bf16[4,256,768]{2,1,0:T(8,128)(2,1)}), bf16[4,256,768]{2,1,0:T(8,128)(2,1)S(1)}, u32[]{:S(2)}, u32[]{:S(2)}) async-start(bf16[4,256,768]{2,1,0:T(8,128)(2,1)} %bitcast.62), calls=%async_computation | async-start | bytes 3145728 | tf_op jit(solution)/shard_map/all_to_all | solution.py:507
  12.8 3.5 copy-start.1
  13.9 43.9 %collective-permute-start.4 = (bf16[192,3072]{1,0:T(8,128)(2,1)}, bf16[192,3072]{1,0:T(8,128)(2,1)}, u32[]{:S(2)}, u32[]{:S(2)}) collective-permute-start(bf16[192,3072]{1,0:T(8,128)(2,1)} %pad_maximum_fusion.a0), channel_id=1, source_target_pairs={{0,2},{1,3},{2,0},{3,1},{4,6},{5,7},{6,4},{7,5},{8,10},{9,11},{10,... | collective-permute-start | bytes 3538952 | tf_op jit(solution)/shard_map/ppermute | solution.py:479
  17.2 59.5 %collective-permute-start.1 = (bf16[192,2304]{1,0:T(8,128)(2,1)}, bf16[192,2304]{1,0:T(8,128)(2,1)}, u32[]{:S(2)}, u32[]{:S(2)}) collective-permute-start(bf16[192,2304]{1,0:T(8,128)(2,1)} %convert_element_type.139.w0), channel_id=1, source_target_pairs={{0,2},{1,3},{2,0},{3,1},{4,6},{5,7},{6,4},{7,5},{8,10},{9,11},{10,... | collective-permute-start | bytes 2654216 | tf_op jit(solution)/shard_map/ppermute | solution.py:479
  18.0 86.3 %collective-permute-start = (bf16[192,2304]{1,0:T(8,128)(2,1)}, bf16[192,2304]{1,0:T(8,128)(2,1)}, u32[]{:S(2)}, u32[]{:S(2)}) collective-permute-start(bf16[192,2304]{1,0:T(8,128)(2,1)} %convert_element_type.139.w0), channel_id=1, source_target_pairs={{0,1},{1,0},{2,3},{3,2},{4,5},{5,4},{6,7},{7,6},{8,9},{9,8},{10,11... | collective-permute-start | bytes 2654216 | tf_op jit(solution)/shard_map/ppermute | solution.py:478
  18.0 128.4 %collective-permute-start.3 = (bf16[192,3072]{1,0:T(8,128)(2,1)}, bf16[192,3072]{1,0:T(8,128)(2,1)}, u32[]{:S(2)}, u32[]{:S(2)}) collective-permute-start(bf16[192,3072]{1,0:T(8,128)(2,1)} %pad_maximum_fusion.a0), channel_id=1, source_target_pairs={{0,1},{1,0},{2,3},{3,2},{4,5},{5,4},{6,7},{7,6},{8,9},{9,8},{10,11... | collective-permute-start | bytes 3538952 | tf_op jit(solution)/shard_map/ppermute | solution.py:478
  32.4 27.4 %copy-start = (bf16[4,256,768]{2,1,0:T(8,128)(2,1)}, bf16[4,256,768]{2,1,0:T(8,128)(2,1)S(1)}, u32[]{:S(2)}) copy-start(bf16[4,256,768]{2,1,0:T(8,128)(2,1)S(1)} %all-to-all-done) | copy-start | bytes 4718596
  32.4 44.3 %copy-start.24 = (f32[2,192]{1,0:T(2,128)S(1)}, f32[2,192]{1,0:T(2,128)}, u32[]{:S(2)}) copy-start(f32[2,192]{1,0:T(2,128)} %param.25) | copy-start | bytes 4612
  32.4 44.4 %copy-start.31 = (s32[2,2]{1,0:T(2,128)S(1)}, s32[2,2]{1,0:T(2,128)}, u32[]{:S(2)}) copy-start(s32[2,2]{1,0:T(2,128)} %param.20) | copy-start | bytes 52
  32.4 114.0 %all-to-all-start.1 = ((bf16[4,256,768]{2,1,0:T(8,128)(2,1)}), bf16[4,256,768]{2,1,0:T(8,128)(2,1)S(1)}, u32[]{:S(2)}, u32[]{:S(2)}) async-start(bf16[4,256,768]{2,1,0:T(8,128)(2,1)} %bitcast.63), calls=%async_computation.1 | async-start | bytes 3145728 | tf_op jit(solution)/shard_map/all_to_all | solution.py:507
  36.1 400.1 %all-reduce.3.cloned.1.call-start = ((), (), s32[]{:S(2)}) async-start(), calls=%async_computation.4 | async-start | bytes 5603328 | tf_op jit(solution)/shard_map/psum | solution.py:544
  57.8 88.6 %collective-permute-start.5 = (bf16[192,3072]{1,0:T(8,128)(2,1)}, bf16[192,3072]{1,0:T(8,128)(2,1)}, u32[]{:S(2)}, u32[]{:S(2)}) collective-permute-start(bf16[192,3072]{1,0:T(8,128)(2,1)} %collective-permute-done.4.a2), channel_id=1, source_target_pairs={{0,1},{1,0},{2,3},{3,2},{4,5},{5,4},{6,7},{7,6},{8,9},{9,8},{10,11... | collective-permute-start | bytes 3538952 | tf_op jit(solution)/shard_map/ppermute | solution.py:480
  59.8 44.1 %collective-permute-start.7 = (bf16[288,768]{1,0:T(8,128)(2,1)}, bf16[288,768]{1,0:T(8,128)(2,1)}, u32[]{:S(2)}, u32[]{:S(2)}) collective-permute-start(bf16[288,768]{1,0:T(8,128)(2,1)} %convert_element_type.142.d0), channel_id=1, source_target_pairs={{0,2},{1,3},{2,0},{3,1},{4,6},{5,7},{6,4},{7,5},{8,10},{9,11},{10,... | collective-permute-start | bytes 1327112 | tf_op jit(solution)/shard_map/ppermute | solution.py:479
  76.8 34.0 %collective-permute-start.2 = (bf16[192,2304]{1,0:T(8,128)(2,1)}, bf16[192,2304]{1,0:T(8,128)(2,1)}, u32[]{:S(2)}, u32[]{:S(2)}) collective-permute-start(bf16[192,2304]{1,0:T(8,128)(2,1)} %collective-permute-done.1.w2), channel_id=1, source_target_pairs={{0,1},{1,0},{2,3},{3,2},{4,5},{5,4},{6,7},{7,6},{8,9},{9,8},{10,11... | collective-permute-start | bytes 2654216 | tf_op jit(solution)/shard_map/ppermute | solution.py:480
  103.9 42.5 %collective-permute-start.6 = (bf16[288,768]{1,0:T(8,128)(2,1)}, bf16[288,768]{1,0:T(8,128)(2,1)}, u32[]{:S(2)}, u32[]{:S(2)}) collective-permute-start(bf16[288,768]{1,0:T(8,128)(2,1)} %convert_element_type.142.d0), channel_id=1, source_target_pairs={{0,1},{1,0},{2,3},{3,2},{4,5},{5,4},{6,7},{7,6},{8,9},{9,8},{10,11... | collective-permute-start | bytes 1327112 | tf_op jit(solution)/shard_map/ppermute | solution.py:478
  104.3 42.1 %collective-permute-start.8 = (bf16[288,768]{1,0:T(8,128)(2,1)}, bf16[288,768]{1,0:T(8,128)(2,1)}, u32[]{:S(2)}, u32[]{:S(2)}) collective-permute-start(bf16[288,768]{1,0:T(8,128)(2,1)} %collective-permute-done.7.d2), channel_id=1, source_target_pairs={{0,1},{1,0},{2,3},{3,2},{4,5},{5,4},{6,7},{7,6},{8,9},{9,8},{10,11... | collective-permute-start | bytes 1327112 | tf_op jit(solution)/shard_map/ppermute | solution.py:480
  146.4 1.1 copy-start.6
  205.4 46.2 %collective-permute-start.9 = (bf16[2,192,768]{2,1,0:T(8,128)(2,1)}, bf16[2,192,768]{2,1,0:T(8,128)(2,1)S(1)}, u32[]{:S(2)}, u32[]{:S(2)}) collective-permute-start(bf16[2,192,768]{2,1,0:T(8,128)(2,1)} %get-tuple-element.54), channel_id=1, source_target_pairs={{0,1},{1,0},{2,3},{3,2},{4,5},{5,4},{6,7},{7,6},{8,9},{9,8},{10,11... | collective-permute-start | bytes 1769480 | tf_op jit(solution)/shard_map/ppermute | solution.py:488
  205.8 51.2 %collective-permute-start.15 = (bf16[2,192,3072]{2,1,0:T(8,128)(2,1)}, bf16[2,192,3072]{2,1,0:T(8,128)(2,1)S(1)}, u32[]{:S(2)}, u32[]{:S(2)}) collective-permute-start(bf16[2,192,3072]{2,1,0:T(8,128)(2,1)} %get-tuple-element.60), channel_id=1, source_target_pairs={{0,1},{1,0},{2,3},{3,2},{4,5},{5,4},{6,7},{7,6},{8,9},{9,8},{10,11... | collective-permute-start | bytes 7077896 | tf_op jit(solution)/shard_map/ppermute | solution.py:488
  226.6 24.5 %copy-start.29 = (bf16[2,288,768]{2,1,0:T(8,128)(2,1)S(1)}, bf16[2,288,768]{2,1,0:T(8,128)(2,1)}, u32[]{:S(2)}) copy-start(bf16[2,288,768]{2,1,0:T(8,128)(2,1)} %get-tuple-element.62) | copy-start | bytes 2654212
  226.6 24.7 %copy-start.30 = (bf16[2,192,768]{2,1,0:T(8,128)(2,1)S(1)}, bf16[2,192,768]{2,1,0:T(8,128)(2,1)}, u32[]{:S(2)}) copy-start(bf16[2,192,768]{2,1,0:T(8,128)(2,1)} %get-tuple-element.56) | copy-start | bytes 1769476
  226.6 25.0 %copy-start.21 = (bf16[2,192,768]{2,1,0:T(8,128)(2,1)S(1)}, bf16[2,192,768]{2,1,0:T(8,128)(2,1)}, u32[]{:S(2)}) copy-start(bf16[2,192,768]{2,1,0:T(8,128)(2,1)} %get-tuple-element.53) | copy-start | bytes 1769476
  250.7 2.3 copy-start.22
  250.7 2.3 collective-permute-start.13
  251.1 5.7 %collective-permute-start.17 = (bf16[2,288,768]{2,1,0:T(8,128)(2,1)S(1)}, bf16[2,288,768]{2,1,0:T(8,128)(2,1)S(1)}, u32[]{:S(2)}, u32[]{:S(2)}) collective-permute-start(bf16[2,288,768]{2,1,0:T(8,128)(2,1)S(1)} %copy-done.29), channel_id=1, source_target_pairs={{0,1},{1,0},{2,3},{3,2},{4,5},{5,4},{6,7},{7,6},{8,9},{9,8},{10,11... | collective-permute-start | bytes 2654216 | tf_op jit(solution)/shard_map/ppermute | solution.py:488
  251.3 3.6 collective-permute-start.11
  251.7 3.1 copy-start.20
  251.8 10.1 %collective-permute-start.10 = (bf16[192,768]{1,0:T(8,128)(2,1)S(1)}, bf16[192,768]{1,0:T(8,128)(2,1)S(1)}, u32[]{:S(2)}, u32[]{:S(2)}) collective-permute-start(bf16[192,768]{1,0:T(8,128)(2,1)S(1)} %slice_bitcast_fusion.8), channel_id=1, source_target_pairs={{0,2},{1,3},{2,0},{3,1},{4,6},{5,7},{6,4},{7,5},{8,10},{9,11},{10,... | collective-permute-start | bytes 884744 | tf_op jit(solution)/shard_map/ppermute | solution.py:489
  253.1 3.7 copy-start.10
  253.1 3.7 copy-start.18
  253.9 14.3 %collective-permute-start.14 = (bf16[192,768]{1,0:T(8,128)(2,1)}, bf16[192,768]{1,0:T(8,128)(2,1)}, u32[]{:S(2)}, u32[]{:S(2)}) collective-permute-start(bf16[192,768]{1,0:T(8,128)(2,1)} %slice_bitcast_fusion.4), channel_id=1, source_target_pairs={{0,2},{1,3},{2,0},{3,1},{4,6},{5,7},{6,4},{7,5},{8,10},{9,11},{10,... | collective-permute-start | bytes 884744 | tf_op jit(solution)/shard_map/ppermute | solution.py:489
  255.0 1.8 copy-start.11
  255.0 2.0 copy-start.9
  255.8 18.7 %collective-permute-start.12 = (bf16[192,768]{1,0:T(8,128)(2,1)}, bf16[192,768]{1,0:T(8,128)(2,1)}, u32[]{:S(2)}, u32[]{:S(2)}) collective-permute-start(bf16[192,768]{1,0:T(8,128)(2,1)} %slice_bitcast_fusion.6), channel_id=1, source_target_pairs={{0,2},{1,3},{2,0},{3,1},{4,6},{5,7},{6,4},{7,5},{8,10},{9,11},{10,... | collective-permute-start | bytes 884744 | tf_op jit(solution)/shard_map/ppermute | solution.py:489
  259.0 51.3 %collective-permute-start.16 = (bf16[192,3072]{1,0:T(8,128)(2,1)}, bf16[192,3072]{1,0:T(8,128)(2,1)}, u32[]{:S(2)}, u32[]{:S(2)}) collective-permute-start(bf16[192,3072]{1,0:T(8,128)(2,1)} %slice_bitcast_fusion), channel_id=1, source_target_pairs={{0,2},{1,3},{2,0},{3,1},{4,6},{5,7},{6,4},{7,5},{8,10},{9,11},{10,... | collective-permute-start | bytes 3538952 | tf_op jit(solution)/shard_map/ppermute | solution.py:489
  260.8 47.6 %collective-permute-start.18 = (bf16[288,768]{1,0:T(8,128)(2,1)}, bf16[288,768]{1,0:T(8,128)(2,1)}, u32[]{:S(2)}, u32[]{:S(2)}) collective-permute-start(bf16[288,768]{1,0:T(8,128)(2,1)} %slice_bitcast_fusion.2), channel_id=1, source_target_pairs={{0,2},{1,3},{2,0},{3,1},{4,6},{5,7},{6,4},{7,5},{8,10},{9,11},{10,... | collective-permute-start | bytes 1327112 | tf_op jit(solution)/shard_map/ppermute | solution.py:489
  313.0 1.4 copy-start.16
  337.7 3.7 copy-start.25
  337.7 3.7 copy-start.26
  337.7 59.5 %copy-start.27 = (f32[2,192]{1,0:T(2,128)S(1)}, f32[2,192]{1,0:T(2,128)}, u32[]{:S(2)}) copy-start(f32[2,192]{1,0:T(2,128)} %param.30) | copy-start | bytes 4612
  337.7 59.5 %copy-start.28 = (f32[2,192]{1,0:T(2,128)S(1)}, f32[2,192]{1,0:T(2,128)}, u32[]{:S(2)}) copy-start(f32[2,192]{1,0:T(2,128)} %param.35) | copy-start | bytes 4612
  337.7 60.1 %all-to-all-start.3 = ((bf16[4,256,768]{2,1,0:T(8,128)(2,1)}), bf16[4,256,768]{2,1,0:T(8,128)(2,1)S(1)}, u32[]{:S(2)}, u32[]{:S(2)}) async-start(bf16[4,256,768]{2,1,0:T(8,128)(2,1)} %bitcast.11), calls=%async_computation.3 | async-start | bytes 3145728 | tf_op jit(solution)/shard_map/all_to_all | solution.py:511
  438.5 1.6 copy-start.17
  440.1 1.1 copy-start.12
  440.2 4.0 copy-start.19
  440.2 4.0 copy-start.23
  440.2 7.3 %copy-start.15 = (f32[192,2304]{1,0:T(8,128)S(1)}, f32[192,2304]{1,0:T(8,128)}, u32[]{:S(2)}) copy-start(f32[192,2304]{1,0:T(8,128)} %param.31) | copy-start | bytes 5308420
  441.2 3.0 copy-start.8
  441.2 6.2 %copy-start.13 = (f32[192,2304]{1,0:T(8,128)S(1)}, f32[192,2304]{1,0:T(8,128)}, u32[]{:S(2)}) copy-start(f32[192,2304]{1,0:T(8,128)} %param.28) | copy-start | bytes 5308420
  441.2 6.2 %copy-start.14 = (f32[192,2304]{1,0:T(8,128)S(1)}, f32[192,2304]{1,0:T(8,128)}, u32[]{:S(2)}) copy-start(f32[192,2304]{1,0:T(8,128)} %param.33) | copy-start | bytes 5308420
  444.2 3.3 copy-start.2
  444.2 3.3 copy-start.4
  444.2 3.3 copy-start.5
  447.5 6.3 %copy-start.7 = (bf16[4,256,768]{2,1,0:T(8,128)(2,1)S(1)}, bf16[4,256,768]{2,1,0:T(8,128)(2,1)}, u32[]{:S(2)}) copy-start(bf16[4,256,768]{2,1,0:T(8,128)(2,1)} %all_to_all.20) | copy-start | bytes 4718596
Sparse Core Ops, SparseCore 0:
  313.2 123.0 all-reduce.2
